TPU v7x, 32 devices: a whole 2x2x4 slice. The times are simulated.
32 devices in a mesh: context: 8 (over y, x, core), tensor: 4 (over z).
Axes of the slice: x: 2, y: 2, z: 4, core: 2. Of those that a mesh axis runs over, the one named last changes fastest.
Arguments:
- activations: bfloat16 [4096, 3072], P('context', 'tensor'), may hold values from -6 to 6
- qkv_weight: bfloat16 [3072, 3, 4096], P(None, None, 'tensor'), may hold values from -0.109375 to 0.109375
- log_decay: float32 [4096, 32], P('context', 'tensor'), may hold values from -1.5 to 0, as said below
- lengths: int32 [8], P('context'), may hold values from 256 to 512, as said below
- out_grad: bfloat16 [4096, 4096], P('context', 'tensor'), may hold values from -0.0014648438 to 0.0014648438
Outputs:
- weight_grad: float32 [3072, 3, 4096], P('context', None, 'tensor')
Inputs may be any that keep to these rules, and one draw needn't show every extreme that they name: `log_decay`: Negative; entries vary from token to token. `lengths`: each entry is a multiple of 256; the live tokens are the first slots of their shard; in every draw at least one shard is full.
All inputs are finite; a program needn't handle non-finite values.
Results may differ from a plain program's by a relative error of at most 0.015.
Values may be sent and summed in bfloat16 or wider, within the bound.
A program may use at most 128 MiB of HBM per device.

v0:
```python
import functools

import jax
import jax.numpy as jnp
from jax import lax
from jax.experimental import pallas as pl
from jax.experimental.pallas import tpu as pltpu
from jax.sharding import PartitionSpec as P


F32 = jnp.float32
BF16 = jnp.bfloat16


def contract(a, b, dims):
    return lax.dot_general(a, b, (dims, ((), ())), preferred_element_type=F32)


ROWS = ((0,), (0,))
LANES = ((1,), (1,))
PLAIN = ((1,), (0,))


def states_kernel(scale, q_ref, k_ref, v_ref, g_ref, c_ref, state_ref, grad_ref):
    c = c_ref[...]
    total = c[-1:, :]
    weighted_k = (k_ref[...].astype(F32) * jnp.exp(total - c)).astype(BF16)
    state_ref[0] = contract(weighted_k, v_ref[...], ROWS).astype(BF16)
    weighted_q = (q_ref[...].astype(F32) * (scale * jnp.exp(c))).astype(BF16)
    grad_ref[0] = contract(weighted_q, g_ref[...], ROWS).astype(BF16)


def intra_kernel(scale, q_ref, k_ref, v_ref, g_ref, c_ref, ct_ref, dq_ref, dk_ref, dv_ref):
    head = pl.program_id(0)
    q, k, v, g = q_ref[...], k_ref[...], v_ref[...], g_ref[...]
    tokens, width = q.shape
    column = jnp.concatenate([c_ref[...]] * (tokens // width), axis=1)
    gap = column - ct_ref[pl.ds(head, 1), :]
    row_at = lax.broadcasted_iota(jnp.int32, (tokens, tokens), 0)
    col_at = lax.broadcasted_iota(jnp.int32, (tokens, tokens), 1)
    decay = jnp.exp(jnp.where(row_at >= col_at, gap, -jnp.inf))
    prob = (contract(q, k, LANES) * scale * decay).astype(BF16)
    score = (contract(g, v, LANES) * decay).astype(BF16)
    dq_ref[...] = scale * contract(score, k, PLAIN)
    dk_ref[...] = scale * contract(score, q, ROWS)
    dv_ref[...] = contract(prob, g, ROWS)


def inter_kernel(scale, len_ref, k_ref, v_ref, g_ref, c_ref, in_ref, later_ref, dq_ref, dk_ref, dv_ref,
                 oq_ref, ok_ref, ov_ref):
    c = c_ref[...]
    live = lax.broadcasted_iota(jnp.int32, c.shape, 0) < len_ref[0]
    until = jnp.exp(c[-1:, :] - c)
    dq = dq_ref[...] + scale * jnp.exp(c) * contract(g_ref[...], in_ref[0], LANES)
    dk = dk_ref[...] + until * contract(v_ref[...], later_ref[0], LANES)
    dv = dv_ref[...] + until * contract(k_ref[...], later_ref[0], PLAIN)
    oq_ref[...] = jnp.where(live, dq, 0.0).astype(BF16)
    ok_ref[...] = jnp.where(live, dk, 0.0).astype(BF16)
    ov_ref[...] = jnp.where(live, dv, 0.0).astype(BF16)


def swap(value, size, distance):
    return lax.ppermute(value, "context", [(i, i ^ distance) for i in range(size)])


PIECES = 4
TILE = 256


def project_kernel(act_ref, live_ref, total_ref, weight_ref, every_ref, q_ref, k_ref, v_ref, totals_ref,
                   weights, sums, own_sem, weight_sem, send_sem, recv_sem, total_send, total_recv):
    size, me = lax.axis_size("tensor"), lax.axis_index("tensor")
    shard_count, shard = lax.axis_size("context"), lax.axis_index("context")
    depth = act_ref.shape[1]
    piece = act_ref.shape[0] // PIECES
    columns = q_ref.shape[1]
    tiles = columns // TILE

    def load(owner, part):
        rows = pl.ds(pl.multiple_of(owner * depth, depth), depth)
        return pltpu.make_async_copy(weight_ref.at[part, rows], weights.at[owner, part], weight_sem.at[owner, part])

    for at in range(size):
        owner = lax.rem(me + at, size)
        for part in range(3):
            load(owner, part).start()

    barrier = pltpu.get_barrier_semaphore()
    for target in (me - 1, me + 1):
        @pl.when((target >= 0) & (target < size))
        def _():
            pl.semaphore_signal(barrier, inc=1, device_id={"tensor": target}, device_id_type=pl.DeviceIdType.MESH)

    @pl.loop(1, shard_count)
    def _(step):
        peer = lax.rem(shard + step, shard_count)
        pl.semaphore_signal(barrier, inc=1, device_id={"context": peer}, device_id_type=pl.DeviceIdType.MESH)

    neighbours = jnp.where(me > 0, 1, 0) + jnp.where(me < size - 1, 1, 0)
    pl.semaphore_wait(barrier, neighbours + shard_count - 1)

    def rows_of(at):
        return pl.ds(pl.multiple_of(at * piece, piece), piece)

    def send(source, owner, at, side):
        return pltpu.make_async_remote_copy(
            src_ref=source,
            dst_ref=every_ref.at[owner, rows_of(at)],
            send_sem=send_sem.at[side, owner, at],
            recv_sem=recv_sem.at[owner, at],
            device_id={"tensor": me + 1 - 2 * side},
            device_id_type=pl.DeviceIdType.MESH,
        )

    def has_target(side):
        target = me + 1 - 2 * side
        return (target >= 0) & (target < size)

    def send_total(step):
        peer = lax.rem(shard + step, shard_count)
        return pltpu.make_async_remote_copy(
            src_ref=total_ref,
            dst_ref=totals_ref.at[shard],
            send_sem=total_send.at[peer],
            recv_sem=total_recv.at[shard],
            device_id={"context": peer},
            device_id_type=pl.DeviceIdType.MESH,
        )

    for at in range(PIECES):
        for side in range(2):
            @pl.when(has_target(side))
            def _():
                send(act_ref.at[rows_of(at)], me, at, side).start()

    @pl.loop(1, shard_count)
    def _(step):
        send_total(step).start()

    own = pltpu.make_async_copy(act_ref, every_ref.at[me], own_sem)
    own.start()
    totals_ref[shard] = total_ref[...]

    for part in range(3):
        load(me, part).wait()

    @pl.loop(0, 3 * tiles)
    def _(tile):
        part = tile // tiles
        cols = pl.ds(pl.multiple_of(lax.rem(tile, tiles) * TILE, TILE), TILE)
        sums[part, :, cols] = jnp.dot(act_ref[...], weights[me, part, :, cols], preferred_element_type=F32)

    own.wait()
    for distance in range(1, size):
        for side in range(2):
            owner = me + (2 * side - 1) * distance

            @pl.when((owner >= 0) & (owner < size))
            def _():
                for part in range(3):
                    load(owner, part).wait()

        @pl.loop(0, PIECES)
        def _(at):
            for side in range(2):
                owner = me + (2 * side - 1) * distance

                @pl.when((owner >= 0) & (owner < size))
                def _():
                    pltpu.make_async_copy(
                        every_ref.at[owner, rows_of(at)], every_ref.at[owner, rows_of(at)], recv_sem.at[owner, at]
                    ).wait()

                    @pl.when(has_target(side))
                    def _():
                        send(every_ref.at[owner, rows_of(at)], owner, at, side).start()

            @pl.loop(0, 2)
            def _(side):
                owner = me + (2 * side - 1) * distance

                @pl.when((owner >= 0) & (owner < size))
                def _():
                    @pl.loop(0, 3 * tiles)
                    def _(tile):
                        part = tile // tiles
                        cols = pl.ds(pl.multiple_of(lax.rem(tile, tiles) * TILE, TILE), TILE)
                        sums[part, rows_of(at), cols] += jnp.dot(
                            every_ref[owner, rows_of(at), :], weights[owner, part, :, cols], preferred_element_type=F32
                        )

    live = live_ref[...]
    for part, ref in enumerate((q_ref, k_ref, v_ref)):
        @pl.loop(0, tiles)
        def _(tile):
            cols = pl.ds(pl.multiple_of(tile * TILE, TILE), TILE)
            ref[:, cols] = (sums[part, :, cols] * live).astype(BF16)

    for side in range(2):
        @pl.when(has_target(side))
        def _():
            for distance in range(size):
                owner = me + (2 * side - 1) * distance

                @pl.when((owner >= 0) & (owner < size))
                def _():
                    for at in range(PIECES):
                        send(every_ref.at[owner, rows_of(at)], owner, at, side).wait_send()

    @pl.loop(1, shard_count)
    def _(step):
        peer = lax.rem(shard + step, shard_count)
        send_total(step).wait_send()
        pltpu.make_async_copy(total_ref, totals_ref.at[peer], total_recv.at[peer]).wait()


def project(activations, weight, live, total, shard_count, size):
    tokens, depth = activations.shape
    columns = weight.shape[2]
    vmem = pl.BlockSpec(memory_space=pltpu.VMEM)
    heads_out = [jax.ShapeDtypeStruct((tokens, columns), BF16)] * 3
    return pl.pallas_call(
        project_kernel,
        in_specs=[vmem] * 3 + [pl.BlockSpec(memory_space=pl.ANY)],
        out_specs=[vmem] * 5,
        out_shape=[jax.ShapeDtypeStruct((size, tokens, depth), BF16)]
        + heads_out
        + [jax.ShapeDtypeStruct((shard_count,) + total.shape, F32)],
        scratch_shapes=[
            pltpu.VMEM((size, 3, depth, columns), BF16),
            pltpu.VMEM((3, tokens, columns), F32),
            pltpu.SemaphoreType.DMA,
            pltpu.SemaphoreType.DMA((size, 3)),
            pltpu.SemaphoreType.DMA((2, size, PIECES)),
            pltpu.SemaphoreType.DMA((size, PIECES)),
            pltpu.SemaphoreType.DMA((shard_count,)),
            pltpu.SemaphoreType.DMA((shard_count,)),
        ],
        compiler_params=pltpu.CompilerParams(collective_id=0, has_side_effects=True, vmem_limit_bytes=48 << 20),
        name="project",
    )(activations, live, total, weight)


def flips(chip):
    bx, by = lax.rem(chip, 2), chip // 2
    return chip + 1 - 2 * bx, chip + 2 - 4 * by, 3 - chip


def fused_kernel(scale, len_ref, act_ref, decay_ref, grad_ref, weight_ref, out_ref,
                 every, decay, run, wide, totals, own_total, qkv, g_ref, sums, rows_ref, acc, own, pair, mixed, mixed_in,
                 prefix, prefix_in, incoming, later,
                 input_sem, weight_sem, send_sem, recv_sem, total_send, total_recv, local_sem, mate_send, mate_recv,
                 row_send, row_recv, own_send, own_recv, mixed_send, mixed_recv, prefix_sem, pair_send, pair_recv,
                 near_send, near_recv, relay_send, relay_recv, hop_send, hop_recv, ready):
    size, me = lax.axis_size("tensor"), lax.axis_index("tensor")
    shard_count, shard = lax.axis_size("context"), lax.axis_index("context")
    core, chip = lax.rem(shard, 2), shard // 2
    others = flips(chip)
    chip_x, chip_y, chip_far = others
    partner = chip * 2 + 1 - core
    is_low = core == 0
    tokens, depth = act_ref.shape
    columns = grad_ref.shape[1]
    heads = decay_ref.shape[0]
    width = columns // heads
    half = heads // 2
    piece = tokens // PIECES
    tiles = columns // TILE
    strip = rows_ref.shape[-1]
    block = tokens // 2
    last = jnp.maximum(me, size - 1 - me)

    def move(source, target, send_at, recv_at, peer):
        return pltpu.make_async_remote_copy(
            src_ref=source, dst_ref=target, send_sem=send_at, recv_sem=recv_at,
            device_id={"context": peer}, device_id_type=pl.DeviceIdType.MESH,
        )

    def rows_of(at):
        return pl.ds(pl.multiple_of(at * piece, piece), piece)

    def cols_of(head):
        return pl.ds(pl.multiple_of(head * width, width), width)

    def strip_of(which):
        return pl.ds(pl.multiple_of(which * strip, strip), strip)

    def at_order(index):
        return lax.rem(core * half + index, heads)

    def send(source, owner, at, side):
        return pltpu.make_async_remote_copy(
            src_ref=source,
            dst_ref=every.at[owner, rows_of(at)],
            send_sem=send_sem.at[side, owner, at],
            recv_sem=recv_sem.at[owner, at],
            device_id={"tensor": me + 1 - 2 * side},
            device_id_type=pl.DeviceIdType.MESH,
        )

    def has_target(side):
        target = me + 1 - 2 * side
        return (target >= 0) & (target < size)

    def send_total(step):
        peer = lax.rem(shard + step, shard_count)
        return move(own_total, totals.at[shard], total_send.at[peer], total_recv.at[shard], peer)

    def keep(source, at, order, which):
        return pltpu.make_async_copy(
            source.at[rows_of(at), strip_of(core)], rows_ref.at[order, which, 0, rows_of(at)], local_sem.at[order, which, at]
        )

    def mate(source, at, order, which):
        return move(
            source.at[rows_of(at), strip_of(1 - core)], rows_ref.at[order, which, 1, rows_of(at)],
            mate_send.at[order, which, at], mate_recv.at[order, which, at], partner,
        )

    def across(source, at, order, which, other):
        target = core + other - 2 * core * other
        return move(
            source.at[rows_of(at), strip_of(target)], rows_ref.at[order, which, 2 + other, rows_of(at)],
            row_send.at[order, which, other, at], row_recv.at[order, which, other, at], others[order] * 2 + target,
        )

    def deliver(source, owner, at):
        for order in range(2):
            near, far = others[order], others[1 - order]

            @pl.when((owner == near) | (owner == chip_far))
            def _():
                which = jnp.where(owner == near, 0, 1)
                for other in range(2):
                    across(source, at, order, which, other).start()

            @pl.when((owner == chip) | (owner == far))
            def _():
                which = jnp.where(owner == chip, 0, 1)
                keep(source, at, order, which).start()
                mate(source, at, order, which).start()

    act_copy = pltpu.make_async_copy(act_ref, every.at[me], input_sem.at[0])
    decay_copy = pltpu.make_async_copy(decay_ref, decay, input_sem.at[1])
    grad_copy = pltpu.make_async_copy(grad_ref, g_ref, input_sem.at[2])

    barrier = pltpu.get_barrier_semaphore()
    for target in (me - 1, me + 1):
        @pl.when((target >= 0) & (target < size))
        def _():
            pl.semaphore_signal(barrier, inc=1, device_id={"tensor": target}, device_id_type=pl.DeviceIdType.MESH)

    @pl.loop(1, shard_count)
    def _(step):
        peer = lax.rem(shard + step, shard_count)
        pl.semaphore_signal(barrier, inc=1, device_id={"context": peer}, device_id_type=pl.DeviceIdType.MESH)

    act_copy.start()
    decay_copy.start()
    act_copy.wait()
    decay_copy.wait()
    neighbours = jnp.where(me > 0, 1, 0) + jnp.where(me < size - 1, 1, 0)
    pl.semaphore_wait(barrier, neighbours + shard_count - 1)

    for at in range(PIECES):
        for side in range(2):
            @pl.when(has_target(side))
            def _():
                send(every.at[me, rows_of(at)], me, at, side).start()

    @pl.loop(0, PIECES)
    def _(at):
        deliver(every.at[me], me, at)

    def running_sums():
        token_at = lax.broadcasted_iota(jnp.int32, (heads, tokens), 1)
        masked = jnp.where(token_at < len_ref[0], decay[...], 0.0)
        row_at = lax.broadcasted_iota(jnp.int32, (tokens, tokens), 0)
        col_at = lax.broadcasted_iota(jnp.int32, (tokens, tokens), 1)
        upto = jnp.where(row_at <= col_at, 1.0, 0.0)
        c = lax.dot_general(
            masked, upto, (PLAIN, ((), ())), precision=lax.Precision.HIGHEST, preferred_element_type=F32
        )
        run[...] = c
        total = c[:, tokens - 1 :].astype(BF16).astype(F32)
        own_total[...] = jnp.broadcast_to(total, own_total.shape)
        totals[shard] = jnp.broadcast_to(total, own_total.shape)
        column = jnp.concatenate([c, jnp.zeros((width - heads, tokens), F32)], axis=0).T
        for head in range(heads):
            wide[head] = jnp.broadcast_to(column[:, head : head + 1], (tokens, width))

    def states(at):
        @pl.loop(0, heads)
        def _(head):
            cols, rows = cols_of(head), rows_of(at)
            c = wide[head, rows, :]
            total = wide[head, tokens - 1 :, :]
            weighted_k = (qkv[1, rows, cols].astype(F32) * jnp.exp(total - c)).astype(BF16)
            acc[0, head] += contract(weighted_k, qkv[2, rows, cols], ROWS)
            weighted_q = (qkv[0, rows, cols].astype(F32) * (scale * jnp.exp(c))).astype(BF16)
            acc[1, head] += contract(weighted_q, g_ref[rows, cols], ROWS)

    def project_all(weights):
        def load(owner, part):
            rows = pl.ds(pl.multiple_of(owner * depth, depth), depth)
            return pltpu.make_async_copy(weight_ref.at[part, rows], weights.at[owner, part], weight_sem.at[owner, part])

        for at in range(size):
            owner = lax.rem(me + at, size)
            for part in range(3):
                load(owner, part).start()
        grad_copy.start()

        running_sums()

        @pl.loop(1, shard_count)
        def _(step):
            send_total(step).start()

        acc[...] = jnp.zeros_like(acc)
        for part in range(3):
            load(me, part).wait()

        def tile_at(tile):
            return tile // tiles, pl.ds(pl.multiple_of(lax.rem(tile, tiles) * TILE, TILE), TILE)

        @pl.loop(0, 3 * tiles)
        def _(tile):
            part, cols = tile_at(tile)
            sums[part, :, cols] = jnp.dot(every[me], weights[me, part, :, cols], preferred_element_type=F32)

        grad_copy.wait()

        for distance in range(1, size):
            for side in range(2):
                owner = me + (2 * side - 1) * distance

                @pl.when((owner >= 0) & (owner < size))
                def _():
                    for part in range(3):
                        load(owner, part).wait()

            @pl.loop(0, PIECES)
            def _(at):
                rows = rows_of(at)
                for side in range(2):
                    owner = me + (2 * side - 1) * distance

                    @pl.when((owner >= 0) & (owner < size))
                    def _():
                        pltpu.make_async_copy(
                            every.at[owner, rows], every.at[owner, rows], recv_sem.at[owner, at]
                        ).wait()

                        @pl.when(has_target(side))
                        def _():
                            send(every.at[owner, rows], owner, at, side).start()

                        deliver(every.at[owner], owner, at)

                @pl.loop(0, 2)
                def _(side):
                    owner = me + (2 * side - 1) * distance
                    valid = (owner >= 0) & (owner < size)

                    def product(part, cols):
                        return sums[part, rows, cols] + jnp.dot(
                            every[owner, rows, :], weights[owner, part, :, cols], preferred_element_type=F32
                        )

                    @pl.when(valid & (distance < last))
                    def _():
                        @pl.loop(0, 3 * tiles)
                        def _(tile):
                            part, cols = tile_at(tile)
                            sums[part, rows, cols] = product(part, cols)

                    if distance >= size // 2:
                        @pl.when(valid & (distance == last))
                        def _():
                            token_at = at * piece + lax.broadcasted_iota(jnp.int32, (piece, TILE), 0)
                            live = token_at < len_ref[0]

                            @pl.loop(0, 3 * tiles)
                            def _(tile):
                                part, cols = tile_at(tile)
                                qkv[part, rows, cols] = jnp.where(live, product(part, cols), 0.0).astype(BF16)

                            states(at)

    pl.run_scoped(project_all, pltpu.VMEM((size, 3, depth, columns), BF16))
    own[...] = acc[...].astype(BF16)

    def half_move(index):
        side = index + core - 2 * index * core
        part = pl.ds((1 - side) * half, half)
        return move(own.at[:, part], pair.at[:, part], own_send.at[index], own_recv.at[index], partner)

    def half_wait(index):
        side = index + core - 2 * index * core
        part = pl.ds(side * half, half)
        pltpu.make_async_copy(pair.at[:, part], pair.at[:, part], own_recv.at[index]).wait()

    def mixed_move(step):
        kind = jnp.where(others[step] > chip, 0, 1)
        return move(mixed.at[kind], mixed_in.at[step], mixed_send.at[step], mixed_recv.at[step], others[step] * 2 + core)

    prefix_move = move(prefix, prefix_in, prefix_sem.at[0], prefix_sem.at[1], partner)

    def total_of(which, head):
        return totals[which, pl.ds(head, 1), :]

    def intra(first, stop):
        @pl.loop(first, stop)
        def _(index):
            head = at_order(index)
            cols = cols_of(head)
            at = [slice(part * block, (part + 1) * block) for part in range(2)]
            q, k, v = [[qkv[part, rows, cols] for rows in at] for part in range(3)]
            g = [g_ref[rows, cols] for rows in at]
            dq, dk, dv = [None] * 2, [None] * 2, [None] * 2

            def add(held, part, value):
                held[part] = value if held[part] is None else held[part] + value

            for t in range(2):
                column = jnp.concatenate([wide[head, at[t], :]] * (block // width), axis=1)
                for s in range(t + 1):
                    gap = column - run[pl.ds(head, 1), at[s]]
                    if s == t:
                        row_at = lax.broadcasted_iota(jnp.int32, (block, block), 0)
                        col_at = lax.broadcasted_iota(jnp.int32, (block, block), 1)
                        gap = jnp.where(row_at >= col_at, gap, -jnp.inf)
                    decayed = jnp.exp(gap)
                    prob = (contract(q[t], k[s], LANES) * scale * decayed).astype(BF16)
                    score = (contract(g[t], v[s], LANES) * decayed).astype(BF16)
                    add(dq, t, contract(score, k[s], PLAIN))
                    add(dk, s, contract(score, q[t], ROWS))
                    add(dv, s, contract(prob, g[t], ROWS))
            for part in range(2):
                sums[0, at[part], cols] = scale * dq[part]
                sums[1, at[part], cols] = scale * dk[part]
                sums[2, at[part], cols] = dv[part]

    def spread(ref, at, head):
        sum_in, sum_later = ref[0, at].astype(F32), ref[1, at].astype(F32)
        incoming[head] = jnp.where(
            is_low, sum_in, jnp.exp(total_of(chip * 2, head)) * sum_in + pair[0, head].astype(F32)
        ).astype(BF16)
        later[head] = jnp.where(
            is_low, jnp.exp(total_of(chip * 2 + 1, head)) * sum_later + pair[1, head].astype(F32), sum_later
        ).astype(BF16)

    def finish_all(grads, hop, hop_in):
        for target in (partner, chip_x * 2 + core, chip_y * 2 + core):
            pl.semaphore_signal(ready, inc=1, device_id={"context": target}, device_id_type=pl.DeviceIdType.MESH)

        for index in range(2):
            half_move(index).start()

        @pl.loop(1, shard_count)
        def _(step):
            peer = lax.rem(shard + step, shard_count)
            pltpu.make_async_copy(own_total, totals.at[peer], total_recv.at[peer]).wait()

        intra(0, FIRST)
        half_wait(0)

        for at in range(half):
            head = core * half + at
            mine, theirs = [[ref[kind, head].astype(F32) for kind in range(2)] for ref in (own, pair)]
            low, high = [
                [jnp.where(is_low == first, mine[kind], theirs[kind]) for kind in range(2)] for first in (True, False)
            ]
            mixed[0, at] = (jnp.exp(total_of(chip * 2 + 1, head)) * low[0] + high[0]).astype(BF16)
            mixed[1, at] = (low[1] + jnp.exp(total_of(chip * 2, head)) * high[1]).astype(BF16)

        for step in (2, 0, 1):
            mixed_move(step).start()

        intra(FIRST, SECOND)
        half_wait(1)
        for step in range(3):
            mixed_move(step).wait_recv()

        for at in range(half):
            head = core * half + at
            sum_in = jnp.zeros((width, width), F32)
            sum_later = jnp.zeros((width, width), F32)
            for step in range(3):
                peer = others[step]
                goes_up = peer > chip
                first = jnp.where(goes_up, chip, peer) * 2 + 1
                stop = jnp.where(goes_up, peer, chip) * 2
                gap = jnp.zeros((1, width), F32)
                for which in range(shard_count):
                    gap = gap + jnp.where((which > first) & (which < stop), total_of(which, head), 0.0)
                term = jnp.exp(gap) * mixed_in[step, at].astype(F32)
                sum_in = sum_in + jnp.where(goes_up, 0.0, term)
                sum_later = sum_later + jnp.where(goes_up, term, 0.0)
            prefix[0, at] = sum_in.astype(BF16)
            prefix[1, at] = sum_later.astype(BF16)

        prefix_move.start()
        for at in range(half):
            spread(prefix, at, core * half + at)
        pl.semaphore_wait(ready, 3)

        def pair_move(head):
            return move(grads.at[head, 0], grads.at[head, 1], pair_send.at[head], pair_recv.at[head], partner)

        def near_move(head):
            near = chip_x + lax.rem(head, 2) * (chip_y - chip_x)
            return move(grads.at[head, 0], grads.at[head, 2], near_send.at[head], near_recv.at[head], near * 2 + core)

        def relay_move(head):
            return move(grads.at[head, 2], grads.at[head, 3], relay_send.at[head], relay_recv.at[head], partner)

        def hop_move(head):
            target = chip_y + lax.rem(head, 2) * (chip_x - chip_y)
            return move(hop.at[head], hop_in.at[head], hop_send.at[head], hop_recv.at[head], target * 2 + core)

        live = lax.broadcasted_iota(jnp.int32, (tokens, width), 0) < len_ref[0]

        def inter(first, stop):
            @pl.loop(first, stop)
            def _(index):
                head = at_order(index)
                cols = cols_of(head)
                c = wide[head]
                until = jnp.exp(wide[head, tokens - 1 :, :] - c)
                k, v, g = qkv[1, :, cols], qkv[2, :, cols], g_ref[:, cols]
                dq = sums[0, :, cols] + scale * jnp.exp(c) * contract(g, incoming[head], LANES)
                dk = sums[1, :, cols] + until * contract(v, later[head], LANES)
                dv = sums[2, :, cols] + until * contract(k, later[head], PLAIN)
                for part, value in enumerate((dq, dk, dv)):
                    grads[head, 0, :, part * width : (part + 1) * width] = jnp.where(live, value, 0.0).astype(BF16)
                near_move(head).start()
                pair_move(head).start()

        inter(0, half)
        intra(SECOND, heads)
        prefix_move.wait_recv()
        for at in range(half):
            spread(prefix_in, at, (1 - core) * half + at)
        inter(half, heads)

        @pl.loop(0, PIECES)
        def _(at):
            for order in range(2):
                for which in range(2):
                    keep(every.at[me], at, order, which).wait()
                    mate(every.at[me], at, order, which).wait_recv()
                    for other in range(2):
                        across(every.at[me], at, order, which, other).wait_recv()

        def product(head, which):
            lhs = rows_ref[lax.rem(head, 2), which].reshape(4 * tokens, strip)
            return contract(lhs, grads[head].reshape(4 * tokens, 3 * width), ROWS)

        def relay(index):
            head = at_order(index)
            near_move(head).wait_recv()
            relay_move(head).start()

        @pl.loop(0, half)
        def _(index):
            relay(index)

        @pl.loop(0, half // 2)
        def _(group):
            for index in range(2):
                relay(half + 2 * group + index)

            def head_at(index):
                return 2 * group + lax.rem(index, 2) + (index // 2) * half

            @pl.loop(0, 4)
            def _(index):
                head = head_at(index)
                pair_move(head).wait_recv()
                relay_move(head).wait_recv()
                hop[head] = product(head, 1).astype(BF16)
                hop_move(head).start()

            @pl.loop(0, 4)
            def _(index):
                head = head_at(index)
                value = product(head, 0)
                for part in range(3):
                    out_ref[part, :, cols_of(head)] = value[:, part * width : (part + 1) * width]

        @pl.loop(0, heads)
        def _(index):
            head = 2 * (index // 4) + lax.rem(index, 2) + (lax.rem(index, 4) // 2) * half
            hop_move(head).wait_recv()
            for part in range(3):
                out_ref[part, :, cols_of(head)] += hop_in[head, :, part * width : (part + 1) * width].astype(F32)

        @pl.loop(0, heads)
        def _(head):
            near_move(head).wait_send()
            pair_move(head).wait_send()
            relay_move(head).wait_send()
            hop_move(head).wait_send()

    pl.run_scoped(
        finish_all,
        pltpu.VMEM((heads, 4, tokens, 3 * width), BF16),
        pltpu.VMEM((heads, strip, 3 * width), BF16),
        pltpu.VMEM((heads, strip, 3 * width), BF16),
    )

    for side in range(2):
        @pl.when(has_target(side))
        def _():
            for distance in range(size):
                owner = me + (2 * side - 1) * distance

                @pl.when((owner >= 0) & (owner < size))
                def _():
                    for at in range(PIECES):
                        send(every.at[owner, rows_of(at)], owner, at, side).wait_send()

    @pl.loop(1, shard_count)
    def _(step):
        send_total(step).wait_send()

    @pl.loop(0, PIECES)
    def _(at):
        for order in range(2):
            for which in range(2):
                mate(every.at[me], at, order, which).wait_send()
                for other in range(2):
                    across(every.at[me], at, order, which, other).wait_send()

    for index in range(2):
        half_move(index).wait_send()
    for step in range(3):
        mixed_move(step).wait_send()
    prefix_move.wait_send()


def fused(scale, lengths, activations, decay, out_grad, weight, shard_count, size):
    tokens, depth = activations.shape
    columns = out_grad.shape[1]
    heads = decay.shape[0]
    width = columns // heads
    half = heads // 2
    strip = size * depth // shard_count
    dma = pltpu.SemaphoreType.DMA
    away = pl.BlockSpec(memory_space=pltpu.HBM)
    return pl.pallas_call(
        functools.partial(fused_kernel, scale),
        in_specs=[pl.BlockSpec(memory_space=pltpu.SMEM)] + [away] * 4,
        out_specs=pl.BlockSpec(memory_space=pltpu.VMEM),
        out_shape=jax.ShapeDtypeStruct((3, strip, columns), F32),
        scratch_shapes=[
            pltpu.VMEM((size, tokens, depth), BF16),
            pltpu.VMEM((heads, tokens), F32),
            pltpu.VMEM((heads, tokens), F32),
            pltpu.VMEM((heads, tokens, width), F32),
            pltpu.VMEM((shard_count, heads, width), F32),
            pltpu.VMEM((heads, width), F32),
            pltpu.VMEM((3, tokens, columns), BF16),
            pltpu.VMEM((tokens, columns), BF16),
            pltpu.VMEM((3, tokens, columns), F32),
            pltpu.VMEM((2, 2, 4, tokens, strip), BF16),
            pltpu.VMEM((2, heads, width, width), F32),
            pltpu.VMEM((2, heads, width, width), BF16),
            pltpu.VMEM((2, heads, width, width), BF16),
            pltpu.VMEM((2, half, width, width), BF16),
            pltpu.VMEM((3, half, width, width), BF16),
            pltpu.VMEM((2, half, width, width), BF16),
            pltpu.VMEM((2, half, width, width), BF16),
            pltpu.VMEM((heads, width, width), BF16),
            pltpu.VMEM((heads, width, width), BF16),
            dma((3,)),
            dma((size, 3)),
            dma((2, size, PIECES)),
            dma((size, PIECES)),
            dma((shard_count,)),
            dma((shard_count,)),
            dma((2, 2, PIECES)),
            dma((2, 2, PIECES)),
            dma((2, 2, PIECES)),
            dma((2, 2, 2, PIECES)),
            dma((2, 2, 2, PIECES)),
            dma((2,)),
            dma((2,)),
            dma((3,)),
            dma((3,)),
            dma((2,)),
        ] + [dma((heads,))] * 8 + [pltpu.SemaphoreType.REGULAR],
        compiler_params=pltpu.CompilerParams(collective_id=1, has_side_effects=True, vmem_limit_bytes=GRANT << 20),
        name="fused",
    )(lengths, activations, decay, out_grad, weight)


FIRST, SECOND = 2, 6
GRANT = 44


def pick(value, bit, mine, me):
    at = (me >> (bit + 1)) & 1
    return lax.dynamic_index_in_dim(value, at if mine else 1 - at, value.ndim - 3 - bit, keepdims=True)


def scatter_sum(lhs, rhs, bits, me, size):
    def times(block):
        flat = block.reshape((-1,) + block.shape[-2:])
        if flat.shape[0] == 1:
            result = contract(flat[0], rhs, ROWS)
        else:
            result = contract(flat, rhs, ((1,), (0,)))
        return result.reshape(block.shape[:-2] + (block.shape[-1], rhs.shape[1]))

    received = []
    keep = lhs
    for bit in bits:
        send = times(pick(keep, bit, False, me))
        for value in received:
            send = send + pick(value, bit, False, me).astype(F32)
        keep = pick(keep, bit, True, me)
        received = [pick(value, bit, True, me) for value in received]
        received.append(swap(send.astype(BF16), size, 2 << bit))
    total = times(keep)
    for value in received:
        total = total + value.astype(F32)
    return total.reshape(lhs.shape[-1], rhs.shape[1])


def is_square(shard_count, size):
    chips = shard_count // 2
    return chips == size and chips.bit_length() - 1 == 2


def shards(activations, qkv_weight, log_decay, lengths, out_grad):
    size = lax.axis_size("context")
    me = lax.axis_index("context")
    core = me & 1
    chip = me >> 1
    chips = size // 2
    tokens = activations.shape[0]
    heads = log_decay.shape[1]
    columns = out_grad.shape[1]
    width = columns // heads
    half = heads // 2
    scale = width ** -0.5

    if is_square(size, lax.axis_size("tensor")):
        return fused(
            scale, lengths, activations, log_decay.T, out_grad, qkv_weight.transpose(1, 0, 2), size, lax.axis_size("tensor")
        ).transpose(1, 0, 2)

    token_at = jnp.arange(tokens, dtype=jnp.int32)
    live = token_at < lengths[0]
    run_sum = jnp.cumsum(log_decay * live.astype(F32)[:, None], axis=0)
    run_wide = jnp.repeat(run_sum, width, axis=1)
    run_rows = run_sum.T
    own_total = run_sum[-1].astype(BF16).astype(F32)
    total_block = jnp.broadcast_to(jnp.pad(own_total, (0, 128 - heads))[None], (8, 128))
    live_column = live.astype(F32)[:, None]
    every, q, k, v, totals = project(
        activations, qkv_weight.transpose(1, 0, 2), live_column, total_block, size, lax.axis_size("tensor")
    )
    totals = totals[:, 0, :heads]

    rows = qkv_weight.shape[0] // size
    blocks = every.shape[2] // (2 * rows)
    low_rows, high_rows = [
        jnp.stack(
            [every[:, :, (2 * at + which) * rows : (2 * at + which + 1) * rows] for at in range(blocks)], axis=1
        ).reshape(chips, tokens, rows)
        for which in (0, 1)
    ]
    own_rows = jnp.where(core == 0, low_rows, high_rows)
    other_rows = swap(jnp.where(core == 0, high_rows, low_rows), size, 1)
    lhs = jnp.concatenate([own_rows, other_rows], axis=1)

    depth = chips.bit_length() - 1
    orders = (tuple(range(depth)), tuple(reversed(range(depth))))
    lhs = lhs.reshape((2,) * depth + lhs.shape[1:])
    lefts = []
    for order in orders:
        if not depth:
            lefts.append(lhs)
            continue
        moved = swap(pick(lhs, order[0], False, me), size, 2 << order[0])
        lefts.append(jnp.concatenate([pick(lhs, order[0], True, me), moved], axis=-2))

    head_spec = pl.BlockSpec((tokens, width), lambda h: (0, h))
    square_spec = pl.BlockSpec((1, width, width), lambda h: (h, 0, 0))
    wide = lambda kind: jax.ShapeDtypeStruct((tokens, columns), kind)
    squares = jax.ShapeDtypeStruct((heads, width, width), BF16)
    state, grad_state = pl.pallas_call(
        functools.partial(states_kernel, scale),
        grid=(heads,),
        in_specs=[head_spec] * 5,
        out_specs=[square_spec] * 2,
        out_shape=[squares] * 2,
        cost_estimate=pl.CostEstimate(flops=4 * tokens * columns * width, bytes_accessed=12 * tokens * columns, transcendentals=0),
        name="states",
    )(q, k, v, out_grad, run_wide)

    both = jnp.stack([state, grad_state])
    other = swap(both, size, 1)
    mine_half = lax.dynamic_slice_in_dim(both, core * half, half, 1).astype(F32)
    other_half = lax.dynamic_slice_in_dim(other, core * half, half, 1).astype(F32)
    pair_totals = lax.dynamic_slice_in_dim(totals, chip * 2, 2, 0)
    pair_half = lax.dynamic_slice_in_dim(pair_totals, core * half, half, 1)
    low, high = [jnp.where(core == which, mine_half, other_half) for which in (0, 1)]
    chip_state = (jnp.exp(pair_half[1])[:, None, None] * low[0] + high[0]).astype(BF16)
    chip_grad = (low[1] + jnp.exp(pair_half[0])[:, None, None] * high[1]).astype(BF16)

    arrivals = [
        swap(jnp.where((chip ^ step) > chip, chip_state, chip_grad), size, 2 * step) for step in range(1, chips)
    ]

    dq, dk, dv = pl.pallas_call(
        functools.partial(intra_kernel, scale),
        grid=(heads,),
        in_specs=[head_spec] * 5 + [pl.BlockSpec((heads, tokens), lambda h: (0, 0))],
        out_specs=[head_spec] * 3,
        out_shape=[wide(F32)] * 3,
        cost_estimate=pl.CostEstimate(
            flops=10 * tokens * tokens * columns, bytes_accessed=24 * tokens * columns, transcendentals=heads * tokens * tokens
        ),
        name="intra",
    )(q, k, v, out_grad, run_wide, run_rows)

    arrivals, dq, dk, dv = lax.optimization_barrier((arrivals, dq, dk, dv))
    upto = jnp.cumsum(totals, axis=0)
    totals_half = lax.dynamic_slice_in_dim(totals, core * half, half, 1)
    upto_half = lax.dynamic_slice_in_dim(upto, core * half, half, 1)
    chip_before = lax.dynamic_index_in_dim(upto_half - totals_half, chip * 2, 0, keepdims=False)
    chip_upto = lax.dynamic_index_in_dim(upto_half, chip * 2 + 1, 0, keepdims=False)
    incoming = jnp.zeros((half, width, width), F32)
    later = jnp.zeros((half, width, width), F32)
    for step in range(1, chips):
        peer = chip ^ step
        goes_up = peer > chip
        arrived = arrivals[step - 1].astype(F32)
        peer_upto = lax.dynamic_index_in_dim(upto_half, peer * 2 + 1, 0, keepdims=False)
        peer_before = lax.dynamic_index_in_dim(upto_half - totals_half, peer * 2, 0, keepdims=False)
        gap = jnp.where(goes_up, peer_before - chip_upto, chip_before - peer_upto)
        term = jnp.exp(gap)[:, None, None] * arrived
        incoming = incoming + jnp.where(goes_up, 0.0, term)
        later = later + jnp.where(goes_up, term, 0.0)
    from_chips = jnp.stack([incoming, later]).astype(BF16)
    other_chips = swap(from_chips, size, 1)
    is_low = core == 0
    from_chips = jnp.concatenate(
        [jnp.where(is_low, from_chips, other_chips), jnp.where(is_low, other_chips, from_chips)], axis=1
    ).astype(F32)
    incoming = jnp.where(
        is_low, from_chips[0], jnp.exp(pair_totals[0])[:, None, None] * from_chips[0] + other[0].astype(F32)
    ).astype(BF16)
    later = jnp.where(
        is_low, jnp.exp(pair_totals[1])[:, None, None] * from_chips[1] + other[1].astype(F32), from_chips[1]
    ).astype(BF16)

    grads = pl.pallas_call(
        functools.partial(inter_kernel, scale),
        grid=(heads,),
        in_specs=[pl.BlockSpec(memory_space=pltpu.SMEM)] + [head_spec] * 4 + [square_spec] * 2 + [head_spec] * 3,
        out_specs=[head_spec] * 3,
        out_shape=[wide(BF16)] * 3,
        cost_estimate=pl.CostEstimate(flops=6 * tokens * columns * width, bytes_accessed=28 * tokens * columns, transcendentals=0),
        name="inter",
    )(lengths, k, v, out_grad, run_wide, incoming, later, dq, dk, dv)

    results = []
    piece = columns // 2
    for part in grads:
        halves = [part[:, :piece], part[:, piece:]]
        if depth:
            moved = [swap(value, size, 2 << order[0]) for value, order in zip(halves, orders)]
            others = swap(jnp.concatenate(moved, axis=1), size, 1)
        partner = swap(part, size, 1)
        pieces = []
        for at, order in enumerate(orders):
            columns_at = slice(at * piece, (at + 1) * piece)
            rhs = [halves[at], partner[:, columns_at]]
            if depth:
                rhs += [moved[at], others[:, columns_at]]
            pieces.append(scatter_sum(lefts[at], jnp.concatenate(rhs, axis=0), order[1:], me, size))
        results.append(jnp.concatenate(pieces, axis=1))
    return jnp.stack(results, axis=1)


def solution(mesh):
    return jax.shard_map(
        shards,
        mesh=mesh,
        in_specs=(
            P("context", "tensor"),
            P(None, None, "tensor"),
            P("context", "tensor"),
            P("context"),
            P("context", "tensor"),
        ),
        out_specs=P("context", None, "tensor"),
        check_vma=False,
    )
```

profile of v0, /device:TPU:0, one launch (start us, length us, event | category | flops | bytes accessed | tf_op | source)
XLA Modules:
  0.0 142.9 jit_solution(13250973569177876583)
XLA Ops:
  0.7 0.0 copy-start
  0.7 1.2 copy-done
  1.9 0.0 copy-start.1
  1.9 1.1 copy-done.1
  3.0 0.0 copy-start.2
  3.0 0.7 copy-done.2
  3.7 137.0 %fused.1 = f32[3,384,1024]{2,1,0:T(8,128)S(1)} custom-call(s32[1]{0:T(128)S(6)} %copy.7.len_ref, bf16[512,768]{1,0:T(8,128)(2,1)S(1)} %copy-done.1, f32[8,512]{1,0:T(8,128)S(1)} %bitcast.4, bf16[512,1024]{1,0:T(8,128)(2,1)S(1)} %copy-done, bf16[3,3072,1024]{2,1,0:T(8,128)(2,1)} %bitcast.5), custom_call_target="tpu_custom_call" | custom-call | tf_op jit(solution)/shard_map/fused/pallas_call | solution.py:753
  140.7 2.2 %copy.8 = f32[384,3,1024]{2,0,1:T(8,128)} copy(f32[384,3,1024]{2,0,1:T(8,128)S(1)} %bitcast.3) | data formatting | bytes 9437184
Async XLA Ops:
  0.7 1.2 copy-start
  1.9 1.1 copy-start.1
  3.0 0.7 copy-start.2
where the time goes:
time: 143 us
  Pallas kernels  137 us (96%)
  local copies, waits for them, and re-layouts  5.26 us (4%)
    pallas_call x1, Pallas kernels, fused(): pl.pallas_call(functools.partial(fused_kernel, scale), in_specs=[pl.Block...  137 us
    unnamed x7, local copies, waits for them, and re-layouts  5.26 us

commit v1 on v0

--- a/solution.py
+++ b/solution.py
@@ -64,7 +64,7 @@
 
 
 PIECES = 4
-TILE = 256
+TILE = 512
 
 
 def project_kernel(act_ref, live_ref, total_ref, weight_ref, every_ref, q_ref, k_ref, v_ref, totals_ref,
@@ -248,10 +248,10 @@
 
 def fused_kernel(scale, len_ref, act_ref, decay_ref, grad_ref, weight_ref, out_ref,
                  every, decay, run, wide, totals, own_total, qkv, g_ref, sums, rows_ref, acc, own, pair, mixed, mixed_in,
-                 prefix, prefix_in, incoming, later,
+                 prefix, prefix_in, incoming, later, detour,
                  input_sem, weight_sem, send_sem, recv_sem, total_send, total_recv, local_sem, mate_send, mate_recv,
                  row_send, row_recv, own_send, own_recv, mixed_send, mixed_recv, prefix_sem, pair_send, pair_recv,
-                 near_send, near_recv, relay_send, relay_recv, hop_send, hop_recv, ready):
+                 near_send, near_recv, relay_send, relay_recv, hop_send, hop_recv, detour_recv, detour_send, ready, opened):
     size, me = lax.axis_size("tensor"), lax.axis_index("tensor")
     shard_count, shard = lax.axis_size("context"), lax.axis_index("context")
     core, chip = lax.rem(shard, 2), shard // 2
@@ -269,6 +269,10 @@
     strip = rows_ref.shape[-1]
     block = tokens // 2
     last = jnp.maximum(me, size - 1 - me)
+    is_end = (me == 0) | (me == size - 1)
+    inward = jnp.where(me == 0, 1, size - 2)
+    is_inner = (me == 1) | (me == size - 2)
+    outward = jnp.where(me == 1, 0, size - 1)
 
     def move(source, target, send_at, recv_at, peer):
         return pltpu.make_async_remote_copy(
@@ -276,6 +280,9 @@
             device_id={"context": peer}, device_id_type=pl.DeviceIdType.MESH,
         )
 
+    def whole(view, sem):
+        return pltpu.make_async_copy(view, view, sem)
+
     def rows_of(at):
         return pl.ds(pl.multiple_of(at * piece, piece), piece)
 
@@ -292,7 +299,7 @@
         return pltpu.make_async_remote_copy(
             src_ref=source,
             dst_ref=every.at[owner, rows_of(at)],
-            send_sem=send_sem.at[side, owner, at],
+            send_sem=send_sem.at[side, owner],
             recv_sem=recv_sem.at[owner, at],
             device_id={"tensor": me + 1 - 2 * side},
             device_id_type=pl.DeviceIdType.MESH,
@@ -304,24 +311,24 @@
 
     def send_total(step):
         peer = lax.rem(shard + step, shard_count)
-        return move(own_total, totals.at[shard], total_send.at[peer], total_recv.at[shard], peer)
+        return move(own_total, totals.at[shard], total_send, total_recv, peer)
 
     def keep(source, at, order, which):
         return pltpu.make_async_copy(
-            source.at[rows_of(at), strip_of(core)], rows_ref.at[order, which, 0, rows_of(at)], local_sem.at[order, which, at]
+            source.at[rows_of(at), strip_of(core)], rows_ref.at[order, which, 0, rows_of(at)], local_sem
         )
 
     def mate(source, at, order, which):
         return move(
             source.at[rows_of(at), strip_of(1 - core)], rows_ref.at[order, which, 1, rows_of(at)],
-            mate_send.at[order, which, at], mate_recv.at[order, which, at], partner,
+            mate_send, mate_recv, partner,
         )
 
     def across(source, at, order, which, other):
         target = core + other - 2 * core * other
         return move(
             source.at[rows_of(at), strip_of(target)], rows_ref.at[order, which, 2 + other, rows_of(at)],
-            row_send.at[order, which, other, at], row_recv.at[order, which, other, at], others[order] * 2 + target,
+            row_send, row_recv, others[order] * 2 + target,
         )
 
     def deliver(source, owner, at):
@@ -355,11 +362,18 @@
         peer = lax.rem(shard + step, shard_count)
         pl.semaphore_signal(barrier, inc=1, device_id={"context": peer}, device_id_type=pl.DeviceIdType.MESH)
 
+    @pl.when(is_inner)
+    def _():
+        for near in (chip_x, chip_y):
+            pl.semaphore_signal(
+                barrier, inc=1, device_id={"context": near * 2 + core, "tensor": outward}, device_id_type=pl.DeviceIdType.MESH
+            )
+
     act_copy.start()
     decay_copy.start()
     act_copy.wait()
     decay_copy.wait()
-    neighbours = jnp.where(me > 0, 1, 0) + jnp.where(me < size - 1, 1, 0)
+    neighbours = jnp.where(me > 0, 1, 0) + jnp.where(me < size - 1, 1, 0) + jnp.where(is_end, 2, 0)
     pl.semaphore_wait(barrier, neighbours + shard_count - 1)
 
     for at in range(PIECES):
@@ -390,7 +404,7 @@
             wide[head] = jnp.broadcast_to(column[:, head : head + 1], (tokens, width))
 
     def states(at):
-        @pl.loop(0, heads)
+        @pl.loop(0, heads, unroll=UNROLL)
         def _(head):
             cols, rows = cols_of(head), rows_of(at)
             c = wide[head, rows, :]
@@ -403,7 +417,10 @@
     def project_all(weights):
         def load(owner, part):
             rows = pl.ds(pl.multiple_of(owner * depth, depth), depth)
-            return pltpu.make_async_copy(weight_ref.at[part, rows], weights.at[owner, part], weight_sem.at[owner, part])
+            return pltpu.make_async_copy(weight_ref.at[part, rows], weights.at[owner, part], weight_sem.at[owner])
+
+        def loaded(owner):
+            return pltpu.make_async_copy(weights.at[owner], weights.at[owner], weight_sem.at[owner])
 
         for at in range(size):
             owner = lax.rem(me + at, size)
@@ -418,8 +435,7 @@
             send_total(step).start()
 
         acc[...] = jnp.zeros_like(acc)
-        for part in range(3):
-            load(me, part).wait()
+        loaded(me).wait()
 
         def tile_at(tile):
             return tile // tiles, pl.ds(pl.multiple_of(lax.rem(tile, tiles) * TILE, TILE), TILE)
@@ -437,8 +453,7 @@
 
                 @pl.when((owner >= 0) & (owner < size))
                 def _():
-                    for part in range(3):
-                        load(owner, part).wait()
+                    loaded(owner).wait()
 
             @pl.loop(0, PIECES)
             def _(at):
@@ -551,17 +566,39 @@
             is_low, jnp.exp(total_of(chip * 2 + 1, head)) * sum_later + pair[1, head].astype(F32), sum_later
         ).astype(BF16)
 
+    def settle():
+        for side in range(2):
+            @pl.when(has_target(side))
+            def _():
+                for distance in range(size):
+                    owner = me + (2 * side - 1) * distance
+
+                    @pl.when((owner >= 0) & (owner < size))
+                    def _():
+                        whole(every.at[owner], send_sem.at[side, owner]).wait()
+
+        whole(totals.at[pl.ds(0, shard_count - 1)], total_send).wait()
+        whole(rows_ref.at[:, :, 1], mate_send).wait()
+        whole(rows_ref.at[:, :, pl.ds(2, 2)], row_send).wait()
+
+        for index in range(2):
+            half_move(index).wait_send()
+        for step in range(3):
+            mixed_move(step).wait_send()
+        prefix_move.wait_send()
+
     def finish_all(grads, hop, hop_in):
         for target in (partner, chip_x * 2 + core, chip_y * 2 + core):
             pl.semaphore_signal(ready, inc=1, device_id={"context": target}, device_id_type=pl.DeviceIdType.MESH)
 
+        @pl.when(is_end)
+        def _():
+            pl.semaphore_signal(opened, inc=1, device_id={"tensor": inward}, device_id_type=pl.DeviceIdType.MESH)
+
         for index in range(2):
             half_move(index).start()
 
-        @pl.loop(1, shard_count)
-        def _(step):
-            peer = lax.rem(shard + step, shard_count)
-            pltpu.make_async_copy(own_total, totals.at[peer], total_recv.at[peer]).wait()
+        whole(totals.at[pl.ds(0, shard_count - 1)], total_recv).wait()
 
         intra(0, FIRST)
         half_wait(0)
@@ -607,18 +644,37 @@
         pl.semaphore_wait(ready, 3)
 
         def pair_move(head):
-            return move(grads.at[head, 0], grads.at[head, 1], pair_send.at[head], pair_recv.at[head], partner)
+            return move(grads.at[head, 0], grads.at[head, 1], pair_send, pair_recv.at[head], partner)
 
         def near_move(head):
             near = chip_x + lax.rem(head, 2) * (chip_y - chip_x)
-            return move(grads.at[head, 0], grads.at[head, 2], near_send.at[head], near_recv.at[head], near * 2 + core)
+            return move(grads.at[head, 0], grads.at[head, 2], near_send, near_recv.at[head], near * 2 + core)
+
+        def out_move(slot):
+            head = at_order(half - 2 + slot)
+            near = chip_x + lax.rem(head, 2) * (chip_y - chip_x)
+            return pltpu.make_async_remote_copy(
+                src_ref=grads.at[head, 0], dst_ref=detour.at[slot], send_sem=near_send, recv_sem=detour_recv.at[slot],
+                device_id={"context": near * 2 + core, "tensor": inward}, device_id_type=pl.DeviceIdType.MESH,
+            )
+
+        def back_move(slot):
+            head = at_order(half - 2 + slot)
+            return pltpu.make_async_remote_copy(
+                src_ref=detour.at[slot], dst_ref=grads.at[head, 2], send_sem=detour_send, recv_sem=near_recv.at[head],
+                device_id={"tensor": outward}, device_id_type=pl.DeviceIdType.MESH,
+            )
+
+        def hand_back(slot):
+            whole(detour.at[slot], detour_recv.at[slot]).wait()
+            back_move(slot).start()
 
         def relay_move(head):
-            return move(grads.at[head, 2], grads.at[head, 3], relay_send.at[head], relay_recv.at[head], partner)
+            return move(grads.at[head, 2], grads.at[head, 3], relay_send, relay_recv.at[head], partner)
 
         def hop_move(head):
             target = chip_y + lax.rem(head, 2) * (chip_x - chip_y)
-            return move(hop.at[head], hop_in.at[head], hop_send.at[head], hop_recv.at[head], target * 2 + core)
+            return move(hop.at[head], hop_in.at[head], hop_send, hop_recv.at[head], target * 2 + core)
 
         live = lax.broadcasted_iota(jnp.int32, (tokens, width), 0) < len_ref[0]
 
@@ -635,7 +691,16 @@
                 dv = sums[2, :, cols] + until * contract(k, later[head], PLAIN)
                 for part, value in enumerate((dq, dk, dv)):
                     grads[head, 0, :, part * width : (part + 1) * width] = jnp.where(live, value, 0.0).astype(BF16)
-                near_move(head).start()
+                around = is_end & (index >= half - 2) & (index < half)
+
+                @pl.when(around)
+                def _():
+                    out_move(index - (half - 2)).start()
+
+                @pl.when(jnp.logical_not(around))
+                def _():
+                    near_move(head).start()
+
                 pair_move(head).start()
 
         inter(0, half)
@@ -645,14 +710,9 @@
             spread(prefix_in, at, (1 - core) * half + at)
         inter(half, heads)
 
-        @pl.loop(0, PIECES)
-        def _(at):
-            for order in range(2):
-                for which in range(2):
-                    keep(every.at[me], at, order, which).wait()
-                    mate(every.at[me], at, order, which).wait_recv()
-                    for other in range(2):
-                        across(every.at[me], at, order, which, other).wait_recv()
+        whole(rows_ref.at[:, :, 0], local_sem).wait()
+        whole(rows_ref.at[:, :, 1], mate_recv).wait()
+        whole(rows_ref.at[:, :, pl.ds(2, 2)], row_recv).wait()
 
         def product(head, which):
             lhs = rows_ref[lax.rem(head, 2), which].reshape(4 * tokens, strip)
@@ -663,14 +723,29 @@
             near_move(head).wait_recv()
             relay_move(head).start()
 
-        @pl.loop(0, half)
-        def _(index):
+        for index in range(half - 2):
             relay(index)
+
+        @pl.when(jnp.logical_not(is_end))
+        def _():
+            for index in (half - 2, half - 1):
+                relay(index)
+
+        @pl.when(is_inner)
+        def _():
+            pl.semaphore_wait(opened, 1)
+            for slot in range(2):
+                hand_back(slot)
 
         @pl.loop(0, half // 2)
         def _(group):
             for index in range(2):
                 relay(half + 2 * group + index)
+
+            @pl.when(is_end & (group == half // 2 - 1))
+            def _():
+                for index in (half - 2, half - 1):
+                    relay(index)
 
             def head_at(index):
                 return 2 * group + lax.rem(index, 2) + (index // 2) * half
@@ -690,6 +765,16 @@
                 for part in range(3):
                     out_ref[part, :, cols_of(head)] = value[:, part * width : (part + 1) * width]
 
+        settle()
+
+        @pl.when(is_inner)
+        def _():
+            whole(detour, detour_send).wait()
+
+        whole(grads.at[:, 0], near_send).wait()
+        whole(grads.at[:, 0], pair_send).wait()
+        whole(grads.at[:, 0], relay_send).wait()
+
         @pl.loop(0, heads)
         def _(index):
             head = 2 * (index // 4) + lax.rem(index, 2) + (lax.rem(index, 4) // 2) * half
@@ -697,12 +782,7 @@
             for part in range(3):
                 out_ref[part, :, cols_of(head)] += hop_in[head, :, part * width : (part + 1) * width].astype(F32)
 
-        @pl.loop(0, heads)
-        def _(head):
-            near_move(head).wait_send()
-            pair_move(head).wait_send()
-            relay_move(head).wait_send()
-            hop_move(head).wait_send()
+        whole(hop, hop_send).wait()
 
     pl.run_scoped(
         finish_all,
@@ -710,35 +790,6 @@
         pltpu.VMEM((heads, strip, 3 * width), BF16),
         pltpu.VMEM((heads, strip, 3 * width), BF16),
     )
-
-    for side in range(2):
-        @pl.when(has_target(side))
-        def _():
-            for distance in range(size):
-                owner = me + (2 * side - 1) * distance
-
-                @pl.when((owner >= 0) & (owner < size))
-                def _():
-                    for at in range(PIECES):
-                        send(every.at[owner, rows_of(at)], owner, at, side).wait_send()
-
-    @pl.loop(1, shard_count)
-    def _(step):
-        send_total(step).wait_send()
-
-    @pl.loop(0, PIECES)
-    def _(at):
-        for order in range(2):
-            for which in range(2):
-                mate(every.at[me], at, order, which).wait_send()
-                for other in range(2):
-                    across(every.at[me], at, order, which, other).wait_send()
-
-    for index in range(2):
-        half_move(index).wait_send()
-    for step in range(3):
-        mixed_move(step).wait_send()
-    prefix_move.wait_send()
 
 
 def fused(scale, lengths, activations, decay, out_grad, weight, shard_count, size):
@@ -775,30 +826,32 @@
             pltpu.VMEM((2, half, width, width), BF16),
             pltpu.VMEM((heads, width, width), BF16),
             pltpu.VMEM((heads, width, width), BF16),
+            pltpu.VMEM((2, tokens, 3 * width), BF16),
             dma((3,)),
-            dma((size, 3)),
-            dma((2, size, PIECES)),
+            dma((size,)),
+            dma((2, size)),
             dma((size, PIECES)),
-            dma((shard_count,)),
-            dma((shard_count,)),
-            dma((2, 2, PIECES)),
-            dma((2, 2, PIECES)),
-            dma((2, 2, PIECES)),
-            dma((2, 2, 2, PIECES)),
-            dma((2, 2, 2, PIECES)),
+            dma,
+            dma,
+            dma,
+            dma,
+            dma,
+            dma,
+            dma,
             dma((2,)),
             dma((2,)),
             dma((3,)),
             dma((3,)),
             dma((2,)),
-        ] + [dma((heads,))] * 8 + [pltpu.SemaphoreType.REGULAR],
+        ] + [dma, dma((heads,))] * 4 + [dma((2,)), dma, pltpu.SemaphoreType.REGULAR, pltpu.SemaphoreType.REGULAR],
         compiler_params=pltpu.CompilerParams(collective_id=1, has_side_effects=True, vmem_limit_bytes=GRANT << 20),
         name="fused",
-    )(lengths, activations, decay, out_grad, weight)
-
-
-FIRST, SECOND = 2, 6
-GRANT = 44
+    )(lengths, *(pltpu.with_memory_space_constraint(value, pltpu.HBM) for value in (activations, decay, out_grad, weight)))
+
+
+FIRST, SECOND = 1, 5
+GRANT = 46
+UNROLL = 4
 
 
 def pick(value, bit, mine, me):
@@ -990,7 +1043,7 @@
 
 
 def solution(mesh):
-    return jax.shard_map(
+    step = jax.shard_map(
         shards,
         mesh=mesh,
         in_specs=(
@@ -1003,3 +1056,6 @@
         out_specs=P("context", None, "tensor"),
         check_vma=False,
     )
+    if is_square(mesh.shape["context"], mesh.shape["tensor"]):
+        return step
+    return step

time: 143 us -> 126 us (0.88)
  Pallas kernels: 137 us -> 123 us
  local copies, waits for them, and re-layouts: 5.26 us -> 2.19 us
    pallas_call x1, Pallas kernels: 137 us -> 123 us  [fused(): pl.pallas_call(functools.partial(fused_kernel, scale), in_specs=[pl.Block...]
    unnamed x7 -> x1, local copies, waits for them, and re-layouts: 5.26 us -> 2.19 us
where the time goes in v1:
time: 126 us
  Pallas kernels  123 us (98%)
  local copies, waits for them, and re-layouts  2.19 us (2%)
    pallas_call x1, Pallas kernels, fused(): pl.pallas_call(functools.partial(fused_kernel, scale), in_specs=[pl.Block...  123 us

profile of v1, /device:TPU:0, one launch (start us, length us, event | category | flops | bytes accessed | tf_op | source)
XLA Modules:
  0.0 126.1 jit_solution(16328684911095384103)
XLA Ops:
  0.7 123.3 %fused.1 = f32[3,384,1024]{2,1,0:T(8,128)S(1)} custom-call(s32[1]{0:T(128)S(6)} %copy.7.len_ref, bf16[512,768]{1,0:T(8,128)(2,1)} %act_ref.1, f32[8,512]{1,0:T(8,128)} %bitcast.5, bf16[512,1024]{1,0:T(8,128)(2,1)} %grad_ref.1, bf16[3,3072,1024]{2,1,0:T(8,128)(2,1)} %bitcast.4), custom_call_target="tpu_custom_call" | custom-call | tf_op jit(solution)/shard_map/fused/pallas_call | solution.py:804
  123.9 2.2 %copy.8 = f32[384,3,1024]{2,0,1:T(8,128)} copy(f32[384,3,1024]{2,0,1:T(8,128)S(1)} %bitcast.3) | data formatting | bytes 9437184

commit v2 on v1

--- a/solution.py
+++ b/solution.py
@@ -371,8 +371,6 @@
 
     act_copy.start()
     decay_copy.start()
-    act_copy.wait()
-    decay_copy.wait()
     neighbours = jnp.where(me > 0, 1, 0) + jnp.where(me < size - 1, 1, 0) + jnp.where(is_end, 2, 0)
     pl.semaphore_wait(barrier, neighbours + shard_count - 1)
 
@@ -380,11 +378,11 @@
         for side in range(2):
             @pl.when(has_target(side))
             def _():
-                send(every.at[me, rows_of(at)], me, at, side).start()
+                send(act_ref.at[rows_of(at)], me, at, side).start()
 
     @pl.loop(0, PIECES)
     def _(at):
-        deliver(every.at[me], me, at)
+        deliver(act_ref, me, at)
 
     def running_sums():
         token_at = lax.broadcasted_iota(jnp.int32, (heads, tokens), 1)
@@ -428,6 +426,7 @@
                 load(owner, part).start()
         grad_copy.start()
 
+        decay_copy.wait()
         running_sums()
 
         @pl.loop(1, shard_count)
@@ -435,6 +434,7 @@
             send_total(step).start()
 
         acc[...] = jnp.zeros_like(acc)
+        act_copy.wait()
         loaded(me).wait()
 
         def tile_at(tile):
@@ -516,9 +516,12 @@
         part = pl.ds(side * half, half)
         pltpu.make_async_copy(pair.at[:, part], pair.at[:, part], own_recv.at[index]).wait()
 
-    def mixed_move(step):
+    def mixed_move(step, part):
         kind = jnp.where(others[step] > chip, 0, 1)
-        return move(mixed.at[kind], mixed_in.at[step], mixed_send.at[step], mixed_recv.at[step], others[step] * 2 + core)
+        at = pl.ds(part * 2, 2)
+        return move(
+            mixed.at[kind, at], mixed_in.at[step, at], mixed_send, mixed_recv.at[step, part], others[step] * 2 + core
+        )
 
     prefix_move = move(prefix, prefix_in, prefix_sem.at[0], prefix_sem.at[1], partner)
 
@@ -583,8 +586,7 @@
 
         for index in range(2):
             half_move(index).wait_send()
-        for step in range(3):
-            mixed_move(step).wait_send()
+        whole(mixed_in, mixed_send).wait()
         prefix_move.wait_send()
 
     def finish_all(grads, hop, hop_in):
@@ -612,36 +614,32 @@
             mixed[0, at] = (jnp.exp(total_of(chip * 2 + 1, head)) * low[0] + high[0]).astype(BF16)
             mixed[1, at] = (low[1] + jnp.exp(total_of(chip * 2, head)) * high[1]).astype(BF16)
 
-        for step in (2, 0, 1):
-            mixed_move(step).start()
-
-        intra(FIRST, SECOND)
-        half_wait(1)
-        for step in range(3):
-            mixed_move(step).wait_recv()
-
-        for at in range(half):
-            head = core * half + at
-            sum_in = jnp.zeros((width, width), F32)
-            sum_later = jnp.zeros((width, width), F32)
+        for part in range(half // 2):
+            for step in (2, 0, 1):
+                mixed_move(step, part).start()
+
+        def gather_states(part):
             for step in range(3):
-                peer = others[step]
-                goes_up = peer > chip
-                first = jnp.where(goes_up, chip, peer) * 2 + 1
-                stop = jnp.where(goes_up, peer, chip) * 2
-                gap = jnp.zeros((1, width), F32)
-                for which in range(shard_count):
-                    gap = gap + jnp.where((which > first) & (which < stop), total_of(which, head), 0.0)
-                term = jnp.exp(gap) * mixed_in[step, at].astype(F32)
-                sum_in = sum_in + jnp.where(goes_up, 0.0, term)
-                sum_later = sum_later + jnp.where(goes_up, term, 0.0)
-            prefix[0, at] = sum_in.astype(BF16)
-            prefix[1, at] = sum_later.astype(BF16)
-
-        prefix_move.start()
-        for at in range(half):
-            spread(prefix, at, core * half + at)
-        pl.semaphore_wait(ready, 3)
+                mixed_move(step, part).wait_recv()
+
+            for at in range(2 * part, 2 * part + 2):
+                head = core * half + at
+                sum_in = jnp.zeros((width, width), F32)
+                sum_later = jnp.zeros((width, width), F32)
+                for step in range(3):
+                    peer = others[step]
+                    goes_up = peer > chip
+                    first = jnp.where(goes_up, chip, peer) * 2 + 1
+                    stop = jnp.where(goes_up, peer, chip) * 2
+                    gap = jnp.zeros((1, width), F32)
+                    for which in range(shard_count):
+                        gap = gap + jnp.where((which > first) & (which < stop), total_of(which, head), 0.0)
+                    term = jnp.exp(gap) * mixed_in[step, at].astype(F32)
+                    sum_in = sum_in + jnp.where(goes_up, 0.0, term)
+                    sum_later = sum_later + jnp.where(goes_up, term, 0.0)
+                prefix[0, at] = sum_in.astype(BF16)
+                prefix[1, at] = sum_later.astype(BF16)
+                spread(prefix, at, head)
 
         def pair_move(head):
             return move(grads.at[head, 0], grads.at[head, 1], pair_send, pair_recv.at[head], partner)
@@ -703,8 +701,16 @@
 
                 pair_move(head).start()
 
-        inter(0, half)
-        intra(SECOND, heads)
+        intra(FIRST, 3)
+        half_wait(1)
+        for part in range(half // 2):
+            gather_states(part)
+            if part == 0:
+                pl.semaphore_wait(ready, 3)
+            inter(2 * part, 2 * part + 2)
+            intra(2 * part + 3, 2 * part + 5)
+        prefix_move.start()
+        intra(half + 3, heads)
         prefix_move.wait_recv()
         for at in range(half):
             spread(prefix_in, at, (1 - core) * half + at)
@@ -840,8 +846,8 @@
             dma,
             dma((2,)),
             dma((2,)),
-            dma((3,)),
-            dma((3,)),
+            dma,
+            dma((3, half // 2)),
             dma((2,)),
         ] + [dma, dma((heads,))] * 4 + [dma((2,)), dma, pltpu.SemaphoreType.REGULAR, pltpu.SemaphoreType.REGULAR],
         compiler_params=pltpu.CompilerParams(collective_id=1, has_side_effects=True, vmem_limit_bytes=GRANT << 20),
@@ -849,7 +855,7 @@
     )(lengths, *(pltpu.with_memory_space_constraint(value, pltpu.HBM) for value in (activations, decay, out_grad, weight)))
 
 
-FIRST, SECOND = 1, 5
+FIRST = 1
 GRANT = 46
 UNROLL = 4
 

time: 126 us -> 124 us (0.984)
  Pallas kernels: 123 us -> 121 us
    pallas_call x1, Pallas kernels: 123 us -> 121 us  [fused(): pl.pallas_call(functools.partial(fused_kernel, scale), in_specs=[pl.Block...]
where the time goes in v2:
time: 124 us; the launch traced here: 123 us
  Pallas kernels  121 us (98%)
  local copies, waits for them, and re-layouts  2.19 us (2%)
    pallas_call x1, Pallas kernels, fused(): pl.pallas_call(functools.partial(fused_kernel, scale), in_specs=[pl.Block...  121 us

profile of v2, /device:TPU:0, one launch (start us, length us, event | category | flops | bytes accessed | tf_op | source)
XLA Modules:
  0.0 123.4 jit_solution(1374949194254215432)
XLA Ops:
  0.7 120.5 %fused.1 = f32[3,384,1024]{2,1,0:T(8,128)S(1)} custom-call(s32[1]{0:T(128)S(6)} %copy.7.len_ref, bf16[512,768]{1,0:T(8,128)(2,1)} %act_ref.1, f32[8,512]{1,0:T(8,128)} %bitcast.5, bf16[512,1024]{1,0:T(8,128)(2,1)} %grad_ref.1, bf16[3,3072,1024]{2,1,0:T(8,128)(2,1)} %bitcast.4), custom_call_target="tpu_custom_call" | custom-call | tf_op jit(solution)/shard_map/fused/pallas_call | solution.py:810
  121.2 2.2 %copy.8 = f32[384,3,1024]{2,0,1:T(8,128)} copy(f32[384,3,1024]{2,0,1:T(8,128)S(1)} %bitcast.3) | data formatting | bytes 9437184

commit v3 on v2

--- a/solution.py
+++ b/solution.py
@@ -248,10 +248,12 @@
 
 def fused_kernel(scale, len_ref, act_ref, decay_ref, grad_ref, weight_ref, out_ref,
                  every, decay, run, wide, totals, own_total, qkv, g_ref, sums, rows_ref, acc, own, pair, mixed, mixed_in,
-                 prefix, prefix_in, incoming, later, detour,
+                 prefix, prefix_in, incoming, later,
+                 run_out, run_near, wide_near, qkv_near, grad_near, ends_near,
                  input_sem, weight_sem, send_sem, recv_sem, total_send, total_recv, local_sem, mate_send, mate_recv,
                  row_send, row_recv, own_send, own_recv, mixed_send, mixed_recv, prefix_sem, pair_send, pair_recv,
-                 near_send, near_recv, relay_send, relay_recv, hop_send, hop_recv, detour_recv, detour_send, ready, opened):
+                 near_send, near_recv, relay_send, relay_recv, hop_send, hop_recv, pass_send, run_send, run_recv,
+                 copy_send, copy_recv, plain_send, plain_recv, ends_send, ends_recv, ready):
     size, me = lax.axis_size("tensor"), lax.axis_index("tensor")
     shard_count, shard = lax.axis_size("context"), lax.axis_index("context")
     core, chip = lax.rem(shard, 2), shard // 2
@@ -270,9 +272,12 @@
     block = tokens // 2
     last = jnp.maximum(me, size - 1 - me)
     is_end = (me == 0) | (me == size - 1)
-    inward = jnp.where(me == 0, 1, size - 2)
     is_inner = (me == 1) | (me == size - 2)
     outward = jnp.where(me == 1, 0, size - 1)
+    far_block = jnp.where(me < size // 2, size - 1, 0)
+
+    def shared(order, side):
+        return half // 2 + order + half * side
 
     def move(source, target, send_at, recv_at, peer):
         return pltpu.make_async_remote_copy(
@@ -328,14 +333,14 @@
         target = core + other - 2 * core * other
         return move(
             source.at[rows_of(at), strip_of(target)], rows_ref.at[order, which, 2 + other, rows_of(at)],
-            row_send, row_recv, others[order] * 2 + target,
+            row_send.at[order, which], row_recv.at[order, which], others[order] * 2 + target,
         )
 
     def deliver(source, owner, at):
         for order in range(2):
             near, far = others[order], others[1 - order]
 
-            @pl.when((owner == near) | (owner == chip_far))
+            @pl.when(((owner == near) | (owner == chip_far)) & jnp.logical_not(is_end & (owner == far_block)))
             def _():
                 which = jnp.where(owner == near, 0, 1)
                 for other in range(2):
@@ -347,6 +352,44 @@
                 keep(source, at, order, which).start()
                 mate(source, at, order, which).start()
 
+    def rows_wait():
+        for order in range(2):
+            for which in range(2):
+                whole(rows_ref.at[order, which, pl.ds(2, 2)], row_recv.at[order, which]).wait()
+
+    def pass_rows():
+        for order in range(2):
+            @pl.when((far_block == chip) | (far_block == others[1 - order]))
+            def _():
+                which = jnp.where(far_block == chip, 0, 1)
+                view = rows_ref.at[order, which, pl.ds(2, 2)]
+                pltpu.make_async_remote_copy(
+                    src_ref=view, dst_ref=view, send_sem=pass_send.at[order], recv_sem=row_recv.at[order, which],
+                    device_id={"tensor": outward}, device_id_type=pl.DeviceIdType.MESH,
+                ).start()
+
+    def grad_share(order, side):
+        return move(
+            grad_ref.at[:, cols_of(shared(order, side))], grad_near.at[2 * order + side], copy_send, copy_recv,
+            others[order] * 2 + core,
+        )
+
+    def run_share(order):
+        return move(run_out, run_near.at[order], run_send, run_recv, others[order] * 2 + core)
+
+    def qkv_share(order, side, at):
+        return move(
+            qkv.at[:, rows_of(at), cols_of(shared(order, side))], qkv_near.at[2 * order + side, :, rows_of(at)],
+            plain_send, plain_recv, others[order] * 2 + core,
+        )
+
+    def ends_share(order, side):
+        for kind, ref in enumerate((incoming, later)):
+            move(
+                ref.at[shared(order, side)], ends_near.at[kind, 2 * order + side], ends_send, ends_recv,
+                others[order] * 2 + core,
+            ).start()
+
     act_copy = pltpu.make_async_copy(act_ref, every.at[me], input_sem.at[0])
     decay_copy = pltpu.make_async_copy(decay_ref, decay, input_sem.at[1])
     grad_copy = pltpu.make_async_copy(grad_ref, g_ref, input_sem.at[2])
@@ -362,16 +405,9 @@
         peer = lax.rem(shard + step, shard_count)
         pl.semaphore_signal(barrier, inc=1, device_id={"context": peer}, device_id_type=pl.DeviceIdType.MESH)
 
-    @pl.when(is_inner)
-    def _():
-        for near in (chip_x, chip_y):
-            pl.semaphore_signal(
-                barrier, inc=1, device_id={"context": near * 2 + core, "tensor": outward}, device_id_type=pl.DeviceIdType.MESH
-            )
-
     act_copy.start()
     decay_copy.start()
-    neighbours = jnp.where(me > 0, 1, 0) + jnp.where(me < size - 1, 1, 0) + jnp.where(is_end, 2, 0)
+    neighbours = jnp.where(me > 0, 1, 0) + jnp.where(me < size - 1, 1, 0)
     pl.semaphore_wait(barrier, neighbours + shard_count - 1)
 
     for at in range(PIECES):
@@ -383,6 +419,12 @@
     @pl.loop(0, PIECES)
     def _(at):
         deliver(act_ref, me, at)
+
+    @pl.when(is_end)
+    def _():
+        for order in range(2):
+            for side in range(2):
+                grad_share(order, side).start()
 
     def running_sums():
         token_at = lax.broadcasted_iota(jnp.int32, (heads, tokens), 1)
@@ -394,6 +436,8 @@
             masked, upto, (PLAIN, ((), ())), precision=lax.Precision.HIGHEST, preferred_element_type=F32
         )
         run[...] = c
+        run_out[0:heads] = c
+        run_out[heads : 2 * heads] = jnp.where(token_at < len_ref[0], 1.0, 0.0)
         total = c[:, tokens - 1 :].astype(BF16).astype(F32)
         own_total[...] = jnp.broadcast_to(total, own_total.shape)
         totals[shard] = jnp.broadcast_to(total, own_total.shape)
@@ -401,9 +445,15 @@
         for head in range(heads):
             wide[head] = jnp.broadcast_to(column[:, head : head + 1], (tokens, width))
 
-    def states(at):
-        @pl.loop(0, heads, unroll=UNROLL)
-        def _(head):
+    def half_move(index):
+        side = index + core - 2 * index * core
+        part = pl.ds((1 - side) * half, half)
+        return move(own.at[:, part], pair.at[:, part], own_send.at[index], own_recv.at[index], partner)
+
+    def states(at, first):
+        @pl.loop(0, half, unroll=UNROLL)
+        def _(index):
+            head = first + index
             cols, rows = cols_of(head), rows_of(at)
             c = wide[head, rows, :]
             total = wide[head, tokens - 1 :, :]
@@ -433,6 +483,11 @@
         def _(step):
             send_total(step).start()
 
+        @pl.when(is_end)
+        def _():
+            for order in range(2):
+                run_share(order).start()
+
         acc[...] = jnp.zeros_like(acc)
         act_copy.wait()
         loaded(me).wait()
@@ -496,20 +551,28 @@
                             token_at = at * piece + lax.broadcasted_iota(jnp.int32, (piece, TILE), 0)
                             live = token_at < len_ref[0]
 
-                            @pl.loop(0, 3 * tiles)
-                            def _(tile):
-                                part, cols = tile_at(tile)
-                                qkv[part, rows, cols] = jnp.where(live, product(part, cols), 0.0).astype(BF16)
-
-                            states(at)
+                            for index in range(2):
+                                first = (1 - core if index == 0 else core) * half
+
+                                @pl.loop(0, 3 * tiles // 2)
+                                def _(tile):
+                                    part, start = tile // (tiles // 2), lax.rem(tile, tiles // 2) * TILE
+                                    cols = pl.ds(pl.multiple_of(first * width + start, width), TILE)
+                                    qkv[part, rows, cols] = jnp.where(live, product(part, cols), 0.0).astype(BF16)
+
+                                states(at, first)
+
+                                @pl.when(is_end)
+                                def _():
+                                    for order in range(2):
+                                        qkv_share(order, 1 - core if index == 0 else core, at).start()
+
+                                @pl.when(at == PIECES - 1)
+                                def _():
+                                    own[:, pl.ds(first, half)] = acc[:, pl.ds(first, half)].astype(BF16)
+                                    half_move(index).start()
 
     pl.run_scoped(project_all, pltpu.VMEM((size, 3, depth, columns), BF16))
-    own[...] = acc[...].astype(BF16)
-
-    def half_move(index):
-        side = index + core - 2 * index * core
-        part = pl.ds((1 - side) * half, half)
-        return move(own.at[:, part], pair.at[:, part], own_send.at[index], own_recv.at[index], partner)
 
     def half_wait(index):
         side = index + core - 2 * index * core
@@ -528,37 +591,79 @@
     def total_of(which, head):
         return totals[which, pl.ds(head, 1), :]
 
+    def within(q, k, v, g, column_at, row_at_block):
+        dq, dk, dv = [None] * 2, [None] * 2, [None] * 2
+
+        def add(held, part, value):
+            held[part] = value if held[part] is None else held[part] + value
+
+        for t in range(2):
+            column = jnp.concatenate([column_at(t)] * (block // width), axis=1)
+            for s in range(t + 1):
+                gap = column - row_at_block(s)
+                if s == t:
+                    row_at = lax.broadcasted_iota(jnp.int32, (block, block), 0)
+                    col_at = lax.broadcasted_iota(jnp.int32, (block, block), 1)
+                    gap = jnp.where(row_at >= col_at, gap, -jnp.inf)
+                decayed = jnp.exp(gap)
+                prob = (contract(q[t], k[s], LANES) * scale * decayed).astype(BF16)
+                score = (contract(g[t], v[s], LANES) * decayed).astype(BF16)
+                add(dq, t, contract(score, k[s], PLAIN))
+                add(dk, s, contract(score, q[t], ROWS))
+                add(dv, s, contract(prob, g[t], ROWS))
+        return [scale * value for value in dq], [scale * value for value in dk], dv
+
+    blocks = [slice(part * block, (part + 1) * block) for part in range(2)]
+
     def intra(first, stop):
         @pl.loop(first, stop)
         def _(index):
             head = at_order(index)
             cols = cols_of(head)
-            at = [slice(part * block, (part + 1) * block) for part in range(2)]
-            q, k, v = [[qkv[part, rows, cols] for rows in at] for part in range(3)]
-            g = [g_ref[rows, cols] for rows in at]
-            dq, dk, dv = [None] * 2, [None] * 2, [None] * 2
-
-            def add(held, part, value):
-                held[part] = value if held[part] is None else held[part] + value
-
-            for t in range(2):
-                column = jnp.concatenate([wide[head, at[t], :]] * (block // width), axis=1)
-                for s in range(t + 1):
-                    gap = column - run[pl.ds(head, 1), at[s]]
-                    if s == t:
-                        row_at = lax.broadcasted_iota(jnp.int32, (block, block), 0)
-                        col_at = lax.broadcasted_iota(jnp.int32, (block, block), 1)
-                        gap = jnp.where(row_at >= col_at, gap, -jnp.inf)
-                    decayed = jnp.exp(gap)
-                    prob = (contract(q[t], k[s], LANES) * scale * decayed).astype(BF16)
-                    score = (contract(g[t], v[s], LANES) * decayed).astype(BF16)
-                    add(dq, t, contract(score, k[s], PLAIN))
-                    add(dk, s, contract(score, q[t], ROWS))
-                    add(dv, s, contract(prob, g[t], ROWS))
-            for part in range(2):
-                sums[0, at[part], cols] = scale * dq[part]
-                sums[1, at[part], cols] = scale * dk[part]
-                sums[2, at[part], cols] = dv[part]
+            q, k, v = [[qkv[part, rows, cols] for rows in blocks] for part in range(3)]
+            g = [g_ref[rows, cols] for rows in blocks]
+            results = within(
+                q, k, v, g, lambda t: wide[head, blocks[t], :], lambda s: run[pl.ds(head, 1), blocks[s]]
+            )
+            for part, values in enumerate(results):
+                for index, value in enumerate(values):
+                    sums[part, blocks[index], cols] = value
+
+    def recompute(relay_move, grads):
+        whole(run_near, run_recv).wait()
+        for order in range(2):
+            column = jnp.concatenate([run_near[order], jnp.zeros((width - 2 * heads, tokens), F32)], axis=0).T
+            for side in range(2):
+                head = shared(order, side)
+                wide_near[2 * order + side] = jnp.broadcast_to(column[:, head : head + 1], (tokens, width))
+            wide_near[4 + order] = jnp.broadcast_to(column[:, heads : heads + 1], (tokens, width))
+        whole(grad_near, copy_recv).wait()
+        whole(qkv_near, plain_recv).wait()
+        whole(ends_near, ends_recv).wait()
+
+        @pl.loop(0, 4)
+        def _(slot):
+            order = slot // 2
+            head = shared(order, lax.rem(slot, 2))
+            q, k, v = [[qkv_near[slot, part, rows, :] for rows in blocks] for part in range(3)]
+            g = [grad_near[slot, rows, :] for rows in blocks]
+            dq, dk, dv = within(
+                q, k, v, g, lambda t: wide_near[slot, blocks[t], :], lambda s: run_near[order, pl.ds(head, 1), blocks[s]]
+            )
+            entering, leaving = ends_near[0, slot], ends_near[1, slot]
+            final = wide_near[slot, tokens - 1 :, :]
+            for part, rows in enumerate(blocks):
+                c = wide_near[slot, rows, :]
+                live = wide_near[4 + order, rows, :] > 0.5
+                until = jnp.exp(final - c)
+                values = (
+                    dq[part] + scale * jnp.exp(c) * contract(g[part], entering, LANES),
+                    dk[part] + until * contract(v[part], leaving, LANES),
+                    dv[part] + until * contract(k[part], leaving, PLAIN),
+                )
+                for at, value in enumerate(values):
+                    grads[head, 2, rows, at * width : (at + 1) * width] = jnp.where(live, value, 0.0).astype(BF16)
+            relay_move(head).start()
 
     def spread(ref, at, head):
         sum_in, sum_later = ref[0, at].astype(F32), ref[1, at].astype(F32)
@@ -582,7 +687,24 @@
 
         whole(totals.at[pl.ds(0, shard_count - 1)], total_send).wait()
         whole(rows_ref.at[:, :, 1], mate_send).wait()
-        whole(rows_ref.at[:, :, pl.ds(2, 2)], row_send).wait()
+        for order in range(2):
+            for which in range(2):
+                block_at = chip_far if which else others[order]
+
+                @pl.when(jnp.logical_not(is_end & (block_at == far_block)))
+                def _():
+                    whole(rows_ref.at[order, which, pl.ds(2, 2)], row_send.at[order, which]).wait()
+
+            @pl.when(is_inner & ((far_block == chip) | (far_block == others[1 - order])))
+            def _():
+                whole(rows_ref.at[order, 0, pl.ds(2, 2)], pass_send.at[order]).wait()
+
+        @pl.when(is_end)
+        def _():
+            whole(run_near, run_send).wait()
+            whole(grad_near, copy_send).wait()
+            whole(qkv_near, plain_send).wait()
+            whole(ends_near, ends_send).wait()
 
         for index in range(2):
             half_move(index).wait_send()
@@ -592,13 +714,6 @@
     def finish_all(grads, hop, hop_in):
         for target in (partner, chip_x * 2 + core, chip_y * 2 + core):
             pl.semaphore_signal(ready, inc=1, device_id={"context": target}, device_id_type=pl.DeviceIdType.MESH)
-
-        @pl.when(is_end)
-        def _():
-            pl.semaphore_signal(opened, inc=1, device_id={"tensor": inward}, device_id_type=pl.DeviceIdType.MESH)
-
-        for index in range(2):
-            half_move(index).start()
 
         whole(totals.at[pl.ds(0, shard_count - 1)], total_recv).wait()
 
@@ -648,25 +763,6 @@
             near = chip_x + lax.rem(head, 2) * (chip_y - chip_x)
             return move(grads.at[head, 0], grads.at[head, 2], near_send, near_recv.at[head], near * 2 + core)
 
-        def out_move(slot):
-            head = at_order(half - 2 + slot)
-            near = chip_x + lax.rem(head, 2) * (chip_y - chip_x)
-            return pltpu.make_async_remote_copy(
-                src_ref=grads.at[head, 0], dst_ref=detour.at[slot], send_sem=near_send, recv_sem=detour_recv.at[slot],
-                device_id={"context": near * 2 + core, "tensor": inward}, device_id_type=pl.DeviceIdType.MESH,
-            )
-
-        def back_move(slot):
-            head = at_order(half - 2 + slot)
-            return pltpu.make_async_remote_copy(
-                src_ref=detour.at[slot], dst_ref=grads.at[head, 2], send_sem=detour_send, recv_sem=near_recv.at[head],
-                device_id={"tensor": outward}, device_id_type=pl.DeviceIdType.MESH,
-            )
-
-        def hand_back(slot):
-            whole(detour.at[slot], detour_recv.at[slot]).wait()
-            back_move(slot).start()
-
         def relay_move(head):
             return move(grads.at[head, 2], grads.at[head, 3], relay_send, relay_recv.at[head], partner)
 
@@ -689,13 +785,8 @@
                 dv = sums[2, :, cols] + until * contract(k, later[head], PLAIN)
                 for part, value in enumerate((dq, dk, dv)):
                     grads[head, 0, :, part * width : (part + 1) * width] = jnp.where(live, value, 0.0).astype(BF16)
-                around = is_end & (index >= half - 2) & (index < half)
-
-                @pl.when(around)
-                def _():
-                    out_move(index - (half - 2)).start()
-
-                @pl.when(jnp.logical_not(around))
+
+                @pl.when(jnp.logical_not(is_end & (lax.rem(index, half) >= half // 2)))
                 def _():
                     near_move(head).start()
 
@@ -707,18 +798,44 @@
             gather_states(part)
             if part == 0:
                 pl.semaphore_wait(ready, 3)
+            if part == half // 2 - 1:
+                @pl.when(is_end)
+                def _():
+                    for order in range(2):
+                        ends_share(order, core)
+
             inter(2 * part, 2 * part + 2)
             intra(2 * part + 3, 2 * part + 5)
+            if part == 0:
+                @pl.when(is_inner)
+                def _():
+                    rows_wait()
+                    pass_rows()
         prefix_move.start()
         intra(half + 3, heads)
         prefix_move.wait_recv()
         for at in range(half):
             spread(prefix_in, at, (1 - core) * half + at)
+
+        @pl.when(is_end)
+        def _():
+            for order in range(2):
+                ends_share(order, 1 - core)
+
         inter(half, heads)
+
+        @pl.when(is_end)
+        def _():
+            recompute(relay_move, grads)
+
 
         whole(rows_ref.at[:, :, 0], local_sem).wait()
         whole(rows_ref.at[:, :, 1], mate_recv).wait()
-        whole(rows_ref.at[:, :, pl.ds(2, 2)], row_recv).wait()
+
+        @pl.when(is_end)
+        def _():
+            rows_wait()
+
 
         def product(head, which):
             lhs = rows_ref[lax.rem(head, 2), which].reshape(4 * tokens, strip)
@@ -729,28 +846,23 @@
             near_move(head).wait_recv()
             relay_move(head).start()
 
-        for index in range(half - 2):
-            relay(index)
-
         @pl.when(jnp.logical_not(is_end))
         def _():
-            for index in (half - 2, half - 1):
+            for index in range(half):
                 relay(index)
 
-        @pl.when(is_inner)
-        def _():
-            pl.semaphore_wait(opened, 1)
-            for slot in range(2):
-                hand_back(slot)
-
         @pl.loop(0, half // 2)
-        def _(group):
-            for index in range(2):
-                relay(half + 2 * group + index)
-
-            @pl.when(is_end & (group == half // 2 - 1))
+        def _(turn):
+            group = jnp.where(is_end, half // 2 - 1 - turn, turn)
+
+            @pl.when(jnp.logical_not(is_end))
             def _():
-                for index in (half - 2, half - 1):
+                for index in range(2):
+                    relay(half + 2 * turn + index)
+
+            @pl.when(is_end & (turn > 0))
+            def _():
+                for index in (0, 1, half, half + 1):
                     relay(index)
 
             def head_at(index):
@@ -773,17 +885,22 @@
 
         settle()
 
-        @pl.when(is_inner)
+        @pl.when(is_end)
         def _():
-            whole(detour, detour_send).wait()
-
-        whole(grads.at[:, 0], near_send).wait()
+            whole(grads.at[pl.ds(0, half), 0], near_send).wait()
+
+        @pl.when(jnp.logical_not(is_end))
+        def _():
+            whole(grads.at[:, 0], near_send).wait()
+
         whole(grads.at[:, 0], pair_send).wait()
         whole(grads.at[:, 0], relay_send).wait()
 
         @pl.loop(0, heads)
         def _(index):
-            head = 2 * (index // 4) + lax.rem(index, 2) + (lax.rem(index, 4) // 2) * half
+            turn = index // 4
+            group = jnp.where(is_end, half // 2 - 1 - turn, turn)
+            head = 2 * group + lax.rem(index, 2) + (lax.rem(index, 4) // 2) * half
             hop_move(head).wait_recv()
             for part in range(3):
                 out_ref[part, :, cols_of(head)] += hop_in[head, :, part * width : (part + 1) * width].astype(F32)
@@ -832,7 +949,12 @@
             pltpu.VMEM((2, half, width, width), BF16),
             pltpu.VMEM((heads, width, width), BF16),
             pltpu.VMEM((heads, width, width), BF16),
-            pltpu.VMEM((2, tokens, 3 * width), BF16),
+            pltpu.VMEM((2 * heads, tokens), F32),
+            pltpu.VMEM((2, 2 * heads, tokens), F32),
+            pltpu.VMEM((6, tokens, width), F32),
+            pltpu.VMEM((4, 3, tokens, width), BF16),
+            pltpu.VMEM((4, tokens, width), BF16),
+            pltpu.VMEM((2, 4, width, width), BF16),
             dma((3,)),
             dma((size,)),
             dma((2, size)),
@@ -842,21 +964,21 @@
             dma,
             dma,
             dma,
-            dma,
-            dma,
+            dma((2, 2)),
+            dma((2, 2)),
             dma((2,)),
             dma((2,)),
             dma,
             dma((3, half // 2)),
             dma((2,)),
-        ] + [dma, dma((heads,))] * 4 + [dma((2,)), dma, pltpu.SemaphoreType.REGULAR, pltpu.SemaphoreType.REGULAR],
+        ] + [dma, dma((heads,))] * 4 + [dma((2,))] + [dma] * 8 + [pltpu.SemaphoreType.REGULAR],
         compiler_params=pltpu.CompilerParams(collective_id=1, has_side_effects=True, vmem_limit_bytes=GRANT << 20),
         name="fused",
     )(lengths, *(pltpu.with_memory_space_constraint(value, pltpu.HBM) for value in (activations, decay, out_grad, weight)))
 
 
 FIRST = 1
-GRANT = 46
+GRANT = 48
 UNROLL = 4
 
 

time: 124 us -> 121 us (0.976)
  Pallas kernels: 121 us -> 117 us
    pallas_call x1, Pallas kernels: 121 us -> 117 us  [fused(): pl.pallas_call(functools.partial(fused_kernel, scale), in_specs=[pl.Block...]
where the time goes in v3:
time: 121 us; the launch traced here: 120 us
  Pallas kernels  117 us (97%)
  local copies, waits for them, and re-layouts  2.19 us (2%)
    pallas_call x1, Pallas kernels, fused(): pl.pallas_call(functools.partial(fused_kernel, scale), in_specs=[pl.Block...  117 us

profile of v3, /device:TPU:0, one launch (start us, length us, event | category | flops | bytes accessed | tf_op | source)
XLA Modules:
  0.0 119.8 jit_solution(11146835289022560032)
XLA Ops:
  0.7 116.9 %fused.1 = f32[3,384,1024]{2,1,0:T(8,128)S(1)} custom-call(s32[1]{0:T(128)S(6)} %copy.7.len_ref, bf16[512,768]{1,0:T(8,128)(2,1)} %act_ref.1, f32[8,512]{1,0:T(8,128)} %bitcast.5, bf16[512,1024]{1,0:T(8,128)(2,1)} %grad_ref.1, bf16[3,3072,1024]{2,1,0:T(8,128)(2,1)} %bitcast.4), custom_call_target="tpu_custom_call" | custom-call | tf_op jit(solution)/shard_map/fused/pallas_call | solution.py:927
  117.6 2.2 %copy.8 = f32[384,3,1024]{2,0,1:T(8,128)} copy(f32[384,3,1024]{2,0,1:T(8,128)S(1)} %bitcast.3) | data formatting | bytes 9437184

commit v4 on v3

--- a/solution.py
+++ b/solution.py
@@ -251,7 +251,7 @@
                  prefix, prefix_in, incoming, later,
                  run_out, run_near, wide_near, qkv_near, grad_near, ends_near,
                  input_sem, weight_sem, send_sem, recv_sem, total_send, total_recv, local_sem, mate_send, mate_recv,
-                 row_send, row_recv, own_send, own_recv, mixed_send, mixed_recv, prefix_sem, pair_send, pair_recv,
+                 row_send, row_recv, own_send, own_recv, mixed_send, mixed_recv, prefix_send, prefix_recv, pair_send, pair_recv,
                  near_send, near_recv, relay_send, relay_recv, hop_send, hop_recv, pass_send, run_send, run_recv,
                  copy_send, copy_recv, plain_send, plain_recv, ends_send, ends_recv, ready):
     size, me = lax.axis_size("tensor"), lax.axis_index("tensor")
@@ -277,7 +277,7 @@
     far_block = jnp.where(me < size // 2, size - 1, 0)
 
     def shared(order, side):
-        return half // 2 + order + half * side
+        return order + half * side
 
     def move(source, target, send_at, recv_at, peer):
         return pltpu.make_async_remote_copy(
@@ -352,10 +352,9 @@
                 keep(source, at, order, which).start()
                 mate(source, at, order, which).start()
 
-    def rows_wait():
+    def rows_wait(which):
         for order in range(2):
-            for which in range(2):
-                whole(rows_ref.at[order, which, pl.ds(2, 2)], row_recv.at[order, which]).wait()
+            whole(rows_ref.at[order, which, pl.ds(2, 2)], row_recv.at[order, which]).wait()
 
     def pass_rows():
         for order in range(2):
@@ -386,7 +385,7 @@
     def ends_share(order, side):
         for kind, ref in enumerate((incoming, later)):
             move(
-                ref.at[shared(order, side)], ends_near.at[kind, 2 * order + side], ends_send, ends_recv,
+                ref.at[shared(order, side)], ends_near.at[side, kind, order], ends_send, ends_recv.at[side],
                 others[order] * 2 + core,
             ).start()
 
@@ -562,7 +561,7 @@
 
                                 states(at, first)
 
-                                @pl.when(is_end)
+                                @pl.when(is_end & ((at < PIECES - 1) | (index == 0)))
                                 def _():
                                     for order in range(2):
                                         qkv_share(order, 1 - core if index == 0 else core, at).start()
@@ -586,7 +585,9 @@
             mixed.at[kind, at], mixed_in.at[step, at], mixed_send, mixed_recv.at[step, part], others[step] * 2 + core
         )
 
-    prefix_move = move(prefix, prefix_in, prefix_sem.at[0], prefix_sem.at[1], partner)
+    def prefix_move(part):
+        at = pl.ds(2 * part, 2)
+        return move(prefix.at[:, at], prefix_in.at[:, at], prefix_send, prefix_recv.at[part], partner)
 
     def total_of(which, head):
         return totals[which, pl.ds(head, 1), :]
@@ -639,31 +640,34 @@
             wide_near[4 + order] = jnp.broadcast_to(column[:, heads : heads + 1], (tokens, width))
         whole(grad_near, copy_recv).wait()
         whole(qkv_near, plain_recv).wait()
-        whole(ends_near, ends_recv).wait()
-
-        @pl.loop(0, 4)
-        def _(slot):
-            order = slot // 2
-            head = shared(order, lax.rem(slot, 2))
-            q, k, v = [[qkv_near[slot, part, rows, :] for rows in blocks] for part in range(3)]
-            g = [grad_near[slot, rows, :] for rows in blocks]
-            dq, dk, dv = within(
-                q, k, v, g, lambda t: wide_near[slot, blocks[t], :], lambda s: run_near[order, pl.ds(head, 1), blocks[s]]
-            )
-            entering, leaving = ends_near[0, slot], ends_near[1, slot]
-            final = wide_near[slot, tokens - 1 :, :]
-            for part, rows in enumerate(blocks):
-                c = wide_near[slot, rows, :]
-                live = wide_near[4 + order, rows, :] > 0.5
-                until = jnp.exp(final - c)
-                values = (
-                    dq[part] + scale * jnp.exp(c) * contract(g[part], entering, LANES),
-                    dk[part] + until * contract(v[part], leaving, LANES),
-                    dv[part] + until * contract(k[part], leaving, PLAIN),
+
+        for index in range(2):
+            side = core if index == 0 else 1 - core
+            whole(ends_near.at[side], ends_recv.at[side]).wait()
+
+            @pl.loop(0, 2)
+            def _(order):
+                slot = 2 * order + side
+                head = shared(order, side)
+                q, k, v = [[qkv_near[slot, part, rows, :] for rows in blocks] for part in range(3)]
+                g = [grad_near[slot, rows, :] for rows in blocks]
+                dq, dk, dv = within(
+                    q, k, v, g, lambda t: wide_near[slot, blocks[t], :], lambda s: run_near[order, pl.ds(head, 1), blocks[s]]
                 )
-                for at, value in enumerate(values):
-                    grads[head, 2, rows, at * width : (at + 1) * width] = jnp.where(live, value, 0.0).astype(BF16)
-            relay_move(head).start()
+                entering, leaving = ends_near[side, 0, order], ends_near[side, 1, order]
+                final = wide_near[slot, tokens - 1 :, :]
+                for part, rows in enumerate(blocks):
+                    c = wide_near[slot, rows, :]
+                    live = wide_near[4 + order, rows, :] > 0.5
+                    until = jnp.exp(final - c)
+                    values = (
+                        dq[part] + scale * jnp.exp(c) * contract(g[part], entering, LANES),
+                        dk[part] + until * contract(v[part], leaving, LANES),
+                        dv[part] + until * contract(k[part], leaving, PLAIN),
+                    )
+                    for at, value in enumerate(values):
+                        grads[head, 2, rows, at * width : (at + 1) * width] = jnp.where(live, value, 0.0).astype(BF16)
+                relay_move(head).start()
 
     def spread(ref, at, head):
         sum_in, sum_later = ref[0, at].astype(F32), ref[1, at].astype(F32)
@@ -709,7 +713,7 @@
         for index in range(2):
             half_move(index).wait_send()
         whole(mixed_in, mixed_send).wait()
-        prefix_move.wait_send()
+        whole(prefix_in, prefix_send).wait()
 
     def finish_all(grads, hop, hop_in):
         for target in (partner, chip_x * 2 + core, chip_y * 2 + core):
@@ -732,6 +736,11 @@
         for part in range(half // 2):
             for step in (2, 0, 1):
                 mixed_move(step, part).start()
+
+        @pl.when(is_end)
+        def _():
+            for order in range(2):
+                qkv_share(order, core, PIECES - 1).start()
 
         def gather_states(part):
             for step in range(3):
@@ -786,41 +795,50 @@
                 for part, value in enumerate((dq, dk, dv)):
                     grads[head, 0, :, part * width : (part + 1) * width] = jnp.where(live, value, 0.0).astype(BF16)
 
-                @pl.when(jnp.logical_not(is_end & (lax.rem(index, half) >= half // 2)))
+                @pl.when(jnp.logical_not(is_end & (lax.rem(index, half) < half // 2)))
                 def _():
                     near_move(head).start()
 
                 pair_move(head).start()
+
+        def gather_others(part):
+            prefix_move(part).wait_recv()
+            for at in range(2 * part, 2 * part + 2):
+                spread(prefix_in, at, (1 - core) * half + at)
 
         intra(FIRST, 3)
         half_wait(1)
         for part in range(half // 2):
             gather_states(part)
+            prefix_move(part).start()
             if part == 0:
                 pl.semaphore_wait(ready, 3)
-            if part == half // 2 - 1:
+
                 @pl.when(is_end)
                 def _():
                     for order in range(2):
                         ends_share(order, core)
 
             inter(2 * part, 2 * part + 2)
+            if part == 0:
+                gather_others(part)
+
+                @pl.when(is_end)
+                def _():
+                    for order in range(2):
+                        ends_share(order, 1 - core)
+
             intra(2 * part + 3, 2 * part + 5)
             if part == 0:
                 @pl.when(is_inner)
                 def _():
-                    rows_wait()
+                    rows_wait(0)
+                    rows_wait(1)
                     pass_rows()
-        prefix_move.start()
+
         intra(half + 3, heads)
-        prefix_move.wait_recv()
-        for at in range(half):
-            spread(prefix_in, at, (1 - core) * half + at)
-
-        @pl.when(is_end)
-        def _():
-            for order in range(2):
-                ends_share(order, 1 - core)
+        for part in range(1, half // 2):
+            gather_others(part)
 
         inter(half, heads)
 
@@ -834,7 +852,7 @@
 
         @pl.when(is_end)
         def _():
-            rows_wait()
+            rows_wait(1)
 
 
         def product(head, which):
@@ -853,7 +871,7 @@
 
         @pl.loop(0, half // 2)
         def _(turn):
-            group = jnp.where(is_end, half // 2 - 1 - turn, turn)
+            group = turn
 
             @pl.when(jnp.logical_not(is_end))
             def _():
@@ -862,7 +880,7 @@
 
             @pl.when(is_end & (turn > 0))
             def _():
-                for index in (0, 1, half, half + 1):
+                for index in (2, 3, half + 2, half + 3):
                     relay(index)
 
             def head_at(index):
@@ -876,12 +894,15 @@
                 hop[head] = product(head, 1).astype(BF16)
                 hop_move(head).start()
 
-            @pl.loop(0, 4)
-            def _(index):
-                head = head_at(index)
-                value = product(head, 0)
-                for part in range(3):
-                    out_ref[part, :, cols_of(head)] = value[:, part * width : (part + 1) * width]
+        @pl.when(is_end)
+        def _():
+            rows_wait(0)
+
+        @pl.loop(0, heads)
+        def _(head):
+            value = product(head, 0)
+            for part in range(3):
+                out_ref[part, :, cols_of(head)] = value[:, part * width : (part + 1) * width]
 
         settle()
 
@@ -898,9 +919,7 @@
 
         @pl.loop(0, heads)
         def _(index):
-            turn = index // 4
-            group = jnp.where(is_end, half // 2 - 1 - turn, turn)
-            head = 2 * group + lax.rem(index, 2) + (lax.rem(index, 4) // 2) * half
+            head = 2 * (index // 4) + lax.rem(index, 2) + (lax.rem(index, 4) // 2) * half
             hop_move(head).wait_recv()
             for part in range(3):
                 out_ref[part, :, cols_of(head)] += hop_in[head, :, part * width : (part + 1) * width].astype(F32)
@@ -954,7 +973,7 @@
             pltpu.VMEM((6, tokens, width), F32),
             pltpu.VMEM((4, 3, tokens, width), BF16),
             pltpu.VMEM((4, tokens, width), BF16),
-            pltpu.VMEM((2, 4, width, width), BF16),
+            pltpu.VMEM((2, 2, 2, width, width), BF16),
             dma((3,)),
             dma((size,)),
             dma((2, size)),
@@ -970,8 +989,9 @@
             dma((2,)),
             dma,
             dma((3, half // 2)),
-            dma((2,)),
-        ] + [dma, dma((heads,))] * 4 + [dma((2,))] + [dma] * 8 + [pltpu.SemaphoreType.REGULAR],
+            dma,
+            dma((half // 2,)),
+        ] + [dma, dma((heads,))] * 4 + [dma((2,))] + [dma] * 7 + [dma((2,))] + [pltpu.SemaphoreType.REGULAR],
         compiler_params=pltpu.CompilerParams(collective_id=1, has_side_effects=True, vmem_limit_bytes=GRANT << 20),
         name="fused",
     )(lengths, *(pltpu.with_memory_space_constraint(value, pltpu.HBM) for value in (activations, decay, out_grad, weight)))

time: 121 us -> 119 us (0.983); the launches traced: 120 us -> 119 us
  no operation moved by 1% of the time
where the time goes in v4:
time: 119 us
  Pallas kernels  116 us (97%)
  local copies, waits for them, and re-layouts  2.19 us (2%)
    pallas_call x1, Pallas kernels, fused(): pl.pallas_call(functools.partial(fused_kernel, scale), in_specs=[pl.Block...  116 us

profile of v4, /device:TPU:0, one launch (start us, length us, event | category | flops | bytes accessed | tf_op | source)
XLA Modules:
  0.0 119.1 jit_solution(168609988939948807)
XLA Ops:
  0.7 116.2 %fused.1 = f32[3,384,1024]{2,1,0:T(8,128)S(1)} custom-call(s32[1]{0:T(128)S(6)} %copy.7.len_ref, bf16[512,768]{1,0:T(8,128)(2,1)} %act_ref.1, f32[8,512]{1,0:T(8,128)} %bitcast.5, bf16[512,1024]{1,0:T(8,128)(2,1)} %grad_ref.1, bf16[3,3072,1024]{2,1,0:T(8,128)(2,1)} %bitcast.4), custom_call_target="tpu_custom_call" | custom-call | tf_op jit(solution)/shard_map/fused/pallas_call | solution.py:946
  116.9 2.2 %copy.8 = f32[384,3,1024]{2,0,1:T(8,128)} copy(f32[384,3,1024]{2,0,1:T(8,128)S(1)} %bitcast.3) | data formatting | bytes 9437184
